TPU v7x, 512 devices: a whole 4x4x16 slice. The times are simulated.
512 devices in a mesh: seq: 128 (over z, y, core), head: 4 (over x).
Axes of the slice: x: 4, y: 4, z: 16, core: 2. Of those that a mesh axis runs over, the one named last changes fastest.
Arguments:
- query_rows: bfloat16 [32768, 4096], P(('seq', 'head')), may hold values from -8 to 8
- key_rows: bfloat16 [32768, 4096], P(('seq', 'head')), may hold values from -8 to 8
- value_rows: bfloat16 [32768, 4096], P(('seq', 'head')), may hold values from -8 to 8
- out_grad: bfloat16 [32768, 4096], P(('seq', 'head')), may hold values from -6 to 6
- clusters: int32 [32, 32768], P('head', 'seq'), may hold values from 0 to 127, as said below
- owner_slot: int32 [32, 128], P('head'), may hold values from 0 to 127, each once within a row
Outputs:
- attn_out: bfloat16 [32768, 4096], P('seq', 'head')
- query_grad: bfloat16 [32768, 4096], P('seq', 'head')
- key_grad: bfloat16 [32768, 4096], P('seq', 'head')
- value_grad: bfloat16 [32768, 4096], P('seq', 'head')
- new_centroids: bfloat16 [32, 128, 128], P('head', 'seq')
Inputs may be any that keep to these rules, and one draw needn't show every extreme that they name: Every one of the 128 clusters holds at least one position in every head. `owner_slot`: each row is a permutation of the 128 rows.
All inputs are finite; a program needn't handle non-finite values.
Results may differ from a plain program's by a relative error of at most 0.023.
Values may be sent and summed in bfloat16 or wider, within the bound.
A program may use at most 128 MiB of HBM per device.

v0:
```python
import jax
import jax.numpy as jnp
from jax import lax
from jax.sharding import PartitionSpec as P

HEAD_DIM = 128
C = 128
WINDOW = 512


def shifted(value, axis, steps):
    count = lax.axis_size(axis)
    first, last = (max(0, -steps), min(count, count - steps))
    return lax.ppermute(value, axis, [(source, source + steps) for source in range(first, last)])


def neighbour(payload, offset):
    return shifted(payload, "seq", offset)


def body(query_rows, key_rows, value_rows, out_grad, clusters, owner_slot):
    query_here, key_here, value_here, grad_here = (
        lax.all_to_all(query_rows, "head", split_axis=1, concat_axis=0, tiled=True),
        lax.all_to_all(key_rows, "head", split_axis=1, concat_axis=0, tiled=True),
        lax.all_to_all(value_rows, "head", split_axis=1, concat_axis=0, tiled=True),
        lax.all_to_all(out_grad, "head", split_axis=1, concat_axis=0, tiled=True),
    )
    tok_rows = query_here.shape[0]
    feat_width = query_here.shape[1]
    head_count = feat_width // HEAD_DIM
    shards = lax.axis_size("seq")
    seq_index = lax.axis_index("seq")
    reach_back = (WINDOW + tok_rows - 2) // tok_rows
    score_scale = HEAD_DIM ** (-0.5)
    queries = query_here.reshape(tok_rows, head_count, HEAD_DIM)
    grad_rows = grad_here.reshape(tok_rows, head_count, HEAD_DIM)
    key_local = key_here.reshape(tok_rows, head_count, HEAD_DIM)
    value_local = value_here.reshape(tok_rows, head_count, HEAD_DIM)
    key_value = jnp.stack((key_here, value_here))
    earlier = [neighbour(key_value, offset) for offset in range(reach_back, 0, -1)]
    window_kv = jnp.concatenate(earlier + [key_value], axis=1)
    span_len = window_kv.shape[1]
    key_win = window_kv[0].reshape(span_len, head_count, HEAD_DIM)
    value_win = window_kv[1].reshape(span_len, head_count, HEAD_DIM)
    query_pos = seq_index * tok_rows + jnp.arange(tok_rows, dtype=jnp.int32)
    key_pos = (seq_index - reach_back) * tok_rows + jnp.arange(span_len, dtype=jnp.int32)
    allowed = (
        (key_pos[None, :] <= query_pos[:, None])
        & (key_pos[None, :] > query_pos[:, None] - WINDOW)
        & (key_pos[None, :] >= 0)
    )
    scores = (
        jnp.einsum("qhd,khd->hqk", queries, key_win, preferred_element_type=jnp.float32)
        * score_scale
    )
    scores = jnp.where(allowed[None], scores, -1e30)
    row_peak = jnp.max(scores, axis=2, keepdims=True)
    exp_scores = jnp.where(allowed[None], jnp.exp(scores - row_peak), 0.0)
    window_probs = exp_scores / jnp.sum(exp_scores, axis=2, keepdims=True)
    probs_low = window_probs.astype(jnp.bfloat16)
    window_out = jnp.einsum(
        "hqk,khd->qhd", probs_low, value_win, preferred_element_type=jnp.float32
    )
    dprobs = jnp.einsum("qhd,khd->hqk", grad_rows, value_win, preferred_element_type=jnp.float32)
    window_delta = jnp.sum(window_probs * dprobs, axis=2, keepdims=True)
    dscores = (window_probs * (dprobs - window_delta) * score_scale).astype(jnp.bfloat16)
    dquery_win = jnp.einsum("hqk,khd->qhd", dscores, key_win, preferred_element_type=jnp.float32)
    dkey_part = jnp.einsum(
        "hqk,qhd->khd", dscores, queries, preferred_element_type=jnp.float32
    ).astype(jnp.bfloat16)
    dvalue_part = jnp.einsum(
        "hqk,qhd->khd", probs_low, grad_rows, preferred_element_type=jnp.float32
    ).astype(jnp.bfloat16)
    part_pair = jnp.stack(
        (dkey_part.reshape(span_len, feat_width), dvalue_part.reshape(span_len, feat_width))
    )
    returned = part_pair[:, reach_back * tok_rows :].astype(jnp.float32)
    for offset in range(1, reach_back + 1):
        first_row = (reach_back - offset) * tok_rows
        returned = returned + neighbour(
            part_pair[:, first_row : first_row + tok_rows], -offset
        ).astype(jnp.float32)
    slot_pick = (owner_slot[:, :, None] == jnp.arange(C, dtype=jnp.int32)[None, None, :]).astype(
        jnp.bfloat16
    )
    cluster_pick = (clusters[:, :, None] == jnp.arange(C, dtype=jnp.int32)[None, None, :]).astype(
        jnp.bfloat16
    )
    members = jnp.einsum(
        "htc,hcr->htr", cluster_pick, slot_pick, preferred_element_type=jnp.float32
    ).astype(jnp.bfloat16)
    query_sums = jnp.einsum("htr,thd->hrd", members, queries, preferred_element_type=jnp.float32)
    grad_sums = jnp.einsum("htr,thd->hrd", members, grad_rows, preferred_element_type=jnp.float32)
    counts = jnp.sum(members.astype(jnp.float32), axis=1)
    per_owner = C // shards
    query_sums, grad_sums, counts = lax.psum((query_sums, grad_sums, counts), "seq")
    centroid = (query_sums / counts[:, :, None]).astype(jnp.bfloat16)
    cluster_grad = grad_sums.astype(jnp.bfloat16)
    owned_rows = lax.dynamic_slice_in_dim(centroid, seq_index * per_owner, per_owner, 1)
    logits = (
        jnp.einsum("hrd,thd->hrt", centroid, key_local, preferred_element_type=jnp.float32)
        * score_scale
    )
    local_peak = jnp.max(logits, axis=2)
    glob_peak = lax.pmax(local_peak, "seq")
    local_exp = jnp.exp(logits - glob_peak[..., None])
    local_mass = jnp.sum(local_exp, axis=2)
    local_weighted = jnp.einsum(
        "hrt,thd->hrd",
        local_exp.astype(jnp.bfloat16),
        value_local,
        preferred_element_type=jnp.float32,
    )
    glob_mass, glob_weighted = lax.psum((local_mass, local_weighted), "seq")
    cluster_out = glob_weighted / glob_mass[..., None]
    weights = local_exp / glob_mass[..., None]
    weights_low = weights.astype(jnp.bfloat16)
    cluster_delta = jnp.sum(cluster_grad.astype(jnp.float32) * cluster_out, axis=2)
    dweights = jnp.einsum(
        "hrd,thd->hrt", cluster_grad, value_local, preferred_element_type=jnp.float32
    )
    dlogits = (weights * (dweights - cluster_delta[..., None]) * score_scale).astype(jnp.bfloat16)
    dkey_cluster = jnp.einsum("hrt,hrd->thd", dlogits, centroid, preferred_element_type=jnp.float32)
    dvalue_cluster = jnp.einsum(
        "hrt,hrd->thd", weights_low, cluster_grad, preferred_element_type=jnp.float32
    )
    spread = jnp.einsum(
        "htr,hrd->thd", members.astype(jnp.float32), cluster_out, precision=lax.Precision.HIGHEST
    )
    attn_out = (window_out + spread).reshape(tok_rows, feat_width).astype(jnp.bfloat16)
    query_grad = dquery_win.reshape(tok_rows, feat_width).astype(jnp.bfloat16)
    key_grad = (returned[0] + dkey_cluster.reshape(tok_rows, feat_width)).astype(jnp.bfloat16)
    value_grad = (returned[1] + dvalue_cluster.reshape(tok_rows, feat_width)).astype(jnp.bfloat16)
    return (attn_out, query_grad, key_grad, value_grad, owned_rows)


def solution(mesh):
    in_specs = (
        P(("seq", "head"), None),
        P(("seq", "head"), None),
        P(("seq", "head"), None),
        P(("seq", "head"), None),
        P("head", "seq"),
        P("head", None),
    )
    out_specs = (
        P("seq", "head"),
        P("seq", "head"),
        P("seq", "head"),
        P("seq", "head"),
        P("head", "seq", None),
    )
    return jax.shard_map(body, mesh=mesh, in_specs=in_specs, out_specs=out_specs, check_vma=False)
```

profile of v0, /device:TPU:1, one launch (start us, length us, event | category | flops | bytes accessed | tf_op | source)
XLA Modules:
  0.0 1490.3 jit_solution(2340496719293820807)
XLA Ops:
  7.2 1.9 copy.170
  9.1 5.0 all-to-all-start.2
  14.1 1.9 copy.172
  16.0 5.1 all-to-all-done.2
  21.0 3.5 all-to-all-start
  24.5 0.8 copy.171
  25.4 0.8 convert_reduce_fusion
  26.2 5.2 all-to-all-done
  31.4 3.5 all-to-all-start.1
  34.9 0.8 copy.169
  35.7 258.0 %psum.36 = f32[8,128]{1,0:T(8,128)S(1)} all-reduce(f32[8,128]{1,0:T(8,128)S(1)} %get-tuple-element.33), channel_id=1, replica_groups=mesh['seq'=128,'head'=4] {'seq'}, use_global_device_ids=true, to_apply=%region_4.5 | all-reduce | flops 1024 | bytes 8192 | tf_op jit(solution)/shard_map/psum | solution.py:96
  293.8 1.0 and_and_fusion
  294.7 0.0 all-to-all-done.1
  294.7 4.5 all-to-all-start.3
  299.2 1.1 pad_maximum_fusion.1
  300.3 1.9 collective-permute-start.1
  302.2 2.3 collective-permute-start
  304.5 0.1 copy.146
  304.6 0.3 copy.116
  304.9 1.1 fusion.72
  306.1 0.0 all-reduce.5.cloned.1.call-update
  306.1 0.0 all-reduce.7.cloned.1.call-start
  306.2 0.9 copy.147
  307.0 0.9 copy.148
  307.9 0.1 copy.149
  308.0 0.0 copy-start.2
  308.1 0.8 copy-done.2
  308.8 0.3 fusion.51
  309.2 331.8 %all-reduce.5.cloned.1.call-done = f32[8,128,128]{2,1,0:T(8,128)} async-done(((f32[8,128,128]{2,1,0:T(8,128)}), f32[8,128,128]{2,1,0:T(8,128)}) %all-reduce.5.cloned.1.call-update) | async-done | bytes 524304 | tf_op jit(solution)/shard_map/psum | solution.py:96
  641.0 1.2 divide_convert_fusion
  642.2 1.4 fusion.70
  643.7 247.9 %pmax.7 = f32[8,128]{1,0:T(8,128)S(1)} all-reduce(f32[8,128]{1,0:T(8,128)S(1)} %get-tuple-element.35), channel_id=1, replica_groups=mesh['seq'=128,'head'=4] {'seq'}, use_global_device_ids=true, to_apply=%region_6.7 | all-reduce | flops 1024 | bytes 8192 | tf_op jit(solution)/shard_map/pmax | solution.py:105
  891.6 0.4 fusion.34
  892.0 2.2 fusion.36
  894.2 0.0 all-reduce.7.cloned.1.call-update
  894.2 492.5 %all-reduce.8 = (f32[8,128]{1,0:T(8,128)S(1)}, bf16[8,128,128]{2,1,0:T(8,128)(2,1)}) all-reduce(f32[8,128]{1,0:T(8,128)S(1)} %fusion.34, f32[8,128,128]{2,1,0:T(8,128)S(1)} %fusion.51), channel_id=1, replica_groups=mesh['seq'=128,'head'=4] {'seq'}, use_global_device_ids=true, to_apply=%region_9.10 | all-reduce | flops 132096 | bytes 794624 | tf_op jit(solution)/shard_map/psum | solution.py:114
  1386.6 2.6 fusion.39
  1389.2 2.6 copy.127
  1391.8 0.6 copy.130
  1392.4 1.5 multiply_reduce_fusion
  1393.9 2.7 fusion.26
  1396.6 2.5 copy.125
  1399.1 2.8 fusion.58
  1401.9 1.7 maximum_maximum_fusion
  1403.7 1.5 fusion.69
  1405.2 1.7 copy.100
  1406.9 1.7 copy.101
  1408.6 4.8 fusion.53
  1413.4 0.0 copy-start.3
  1413.4 6.9 fusion.71
  1420.2 5.1 convolution_convert_fusion
  1425.3 11.3 fusion.12
  1436.6 1.7 copy.119
  1438.3 1.7 copy.120
  1440.1 1.5 fusion.27
  1441.6 1.4 collective-permute-start.3
  1443.0 8.4 collective-permute-start.2
  1451.4 4.3 fusion.21
  1455.7 2.0 copy.128
  1457.7 11.5 fusion.24
  1469.3 2.0 copy.129
  1471.3 8.7 collective-permute-done.2
  1480.0 2.1 convert_add_fusion
  1482.1 1.3 fusion.30
  (37 shorter events, 0.1 us)
Async XLA Ops:
  7.2 17.3 %copy-start.9 = (bf16[64,4096]{1,0:T(8,128)(2,1)S(1)}, bf16[64,4096]{1,0:T(8,128)(2,1)}, u32[]{:S(2)}) copy-start(bf16[64,4096]{1,0:T(8,128)(2,1)} %param.8) | copy-start | bytes 1572868
  7.2 18.2 %copy-start.13 = (s32[8,128]{1,0:T(8,128)S(1)}, s32[8,128]{1,0:T(8,128)}, u32[]{:S(2)}) copy-start(s32[8,128]{1,0:T(8,128)} %param.11) | copy-start | bytes 12292
  7.2 18.2 %copy-start.12 = (s32[8,256]{1,0:T(8,128)S(1)}, s32[8,256]{1,0:T(8,128)}, u32[]{:S(2)}) copy-start(s32[8,256]{1,0:T(8,128)} %param.10) | copy-start | bytes 24580
  9.1 25.8 %copy-start.10 = (bf16[64,4096]{1,0:T(8,128)(2,1)S(1)}, bf16[64,4096]{1,0:T(8,128)(2,1)}, u32[]{:S(2)}) copy-start(bf16[64,4096]{1,0:T(8,128)(2,1)} %param.9) | copy-start | bytes 1572868
  9.1 11.9 all-to-all-start.2
  21.0 10.4 all-to-all-start
  31.4 263.3 %all-to-all-start.1 = ((bf16[64,4,1024]{2,0,1:T(8,128)(2,1)}), bf16[64,4,1024]{2,0,1:T(8,128)(2,1)S(1)}, u32[]{:S(2)}, u32[]{:S(2)}) async-start(bf16[64,4,1024]{2,0,1:T(8,128)(2,1)} %bitcast.123), calls=%async_computation.1 | async-start | bytes 1048576 | tf_op jit(solution)/shard_map/all_to_all | solution.py:25
  294.7 13.2 all-to-all-start.3
  299.2 341.8 %all-reduce.5.cloned.1.call-start = ((), (), s32[]{:S(2)}) async-start(), calls=%async_computation.4 | async-start | bytes 1048576 | tf_op jit(solution)/shard_map/psum | solution.py:96
  300.3 1101.6 %collective-permute-start.1 = (bf16[2,256,1024]{2,1,0:T(8,128)(2,1)}, bf16[2,256,1024]{2,1,0:T(8,128)(2,1)}, u32[]{:S(2)}, u32[]{:S(2)}) collective-permute-start(bf16[2,256,1024]{2,1,0:T(8,128)(2,1)} %pad_maximum_fusion.1), channel_id=1, source_target_pairs={{0,4},{4,8},{8,12},{12,16},{16,20},{20,24},{24,28},{28,32},{32,36}... | collective-permute-start | bytes 3145736 | tf_op jit(solution)/shard_map/ppermute | solution.py:14
  302.2 1099.7 %collective-permute-start = (bf16[2,256,1024]{2,1,0:T(8,128)(2,1)}, bf16[2,256,1024]{2,1,0:T(8,128)(2,1)}, u32[]{:S(2)}, u32[]{:S(2)}) collective-permute-start(bf16[2,256,1024]{2,1,0:T(8,128)(2,1)} %pad_maximum_fusion.1), channel_id=1, source_target_pairs={{0,8},{4,12},{8,16},{12,20},{16,24},{20,28},{24,32},{28,36},{32,40... | collective-permute-start | bytes 3145736 | tf_op jit(solution)/shard_map/ppermute | solution.py:14
  304.9 4.3 copy-start.6
  306.1 1086.3 %all-reduce.7.cloned.1.call-start = ((), (), s32[]{:S(2)}) async-start(), calls=%async_computation.5 | async-start | bytes 1048576 | tf_op jit(solution)/shard_map/psum | solution.py:114
  308.0 0.8 copy-start.2
  1386.6 7.2 copy-start.8
  1406.9 6.5 copy-start
  1408.6 4.8 copy-start.7
  1408.6 4.8 copy-start.11
  1413.4 6.9 copy-start.3
  1440.1 11.3 copy-start.1
  1440.1 11.3 copy-start.14
  1441.6 29.8 %collective-permute-start.3 = (bf16[2,256,1024]{2,1,0:T(8,128)(2,1)}, bf16[2,256,1024]{2,1,0:T(8,128)(2,1)}, u32[]{:S(2)}, u32[]{:S(2)}) collective-permute-start(bf16[2,256,1024]{2,1,0:T(8,128)(2,1)} %get-tuple-element.28), channel_id=1, source_target_pairs={{8,0},{12,4},{16,8},{20,12},{24,16},{28,20},{32,24},{36,28},{40,32... | collective-permute-start | bytes 3145736 | tf_op jit(solution)/shard_map/ppermute | solution.py:14
  1443.0 37.0 %collective-permute-start.2 = (bf16[2,256,1024]{2,1,0:T(8,128)(2,1)}, bf16[2,256,1024]{2,1,0:T(8,128)(2,1)}, u32[]{:S(2)}, u32[]{:S(2)}) collective-permute-start(bf16[2,256,1024]{2,1,0:T(8,128)(2,1)} %get-tuple-element.27), channel_id=1, source_target_pairs={{4,0},{8,4},{12,8},{16,12},{20,16},{24,20},{28,24},{32,28},{36,32}... | collective-permute-start | bytes 3145736 | tf_op jit(solution)/shard_map/ppermute | solution.py:14
  1471.3 10.8 copy-start.4
  1471.3 10.8 copy-start.5
Sparse Core Ops, SparseCore 0:
  306.2 334.7 all-reduce.4
  894.3 333.2 all-reduce.6
where the time goes:
time: 1500 us; the launch traced here: 1490 us
  blocking collectives  998 us (67%)
  waiting for transfers between devices  351 us (23%)
  matrix products  57.9 us (4%)
  starting transfers between devices  30.4 us (2%)
  local copies, waits for them, and re-layouts  26.7 us (2%)
    psum x1, blocking collectives, body(): glob_mass, glob_weighted = lax.psum((local_mass, local_weighted), 'seq')  492 us
    psum x1, waiting for transfers between devices, body(): lax.psum((query_sums, grad_sums, counts), 'seq')  332 us
    psum x1, blocking collectives, body(): lax.psum((query_sums, grad_sums, counts), 'seq')  258 us
    pmax x1, blocking collectives, body(): glob_peak = lax.pmax(local_peak, 'seq')  248 us
  transfers between devices with their start and end apart: 10, of which 4 were waited for; matrix products, arithmetic and copies ran while one was open for 3% of the time, Pallas kernels for 0%

commit v1 on v0

v1 whole, which is shorter than its diff:
```python
import functools

import jax
import jax.numpy as jnp
from jax import lax
from jax.experimental import pallas as pl
from jax.experimental.pallas import tpu as pltpu
from jax.sharding import PartitionSpec as P

HEAD_DIM = 128
WINDOW = 512
F32 = jnp.float32
BF16 = jnp.bfloat16
NN = (((1,), (0,)), ((), ()))
NT = (((1,), (1,)), ((), ()))
TN = (((0,), (0,)), ((), ()))


def factors(count):
    return {128: (16, 4, 2), 8: (2, 2, 2)}[count]


def mm(a, b, dims):
    return lax.dot_general(a, b, dims, preferred_element_type=F32)


def pick(table, lane):
    lanes = lax.broadcasted_iota(jnp.int32, table.shape, 1)
    return jnp.sum(jnp.where(lanes == lane, table, 0.0), axis=1, keepdims=True)


def kernel(
    dims, q_in, k_in, v_in, g_in, clus, slot, attn_out, dq_out, dk_out, dv_out, cent_out,
    qb, gb, kw, vw, part, ret, mem, wout, bias,
    cnt, cnt_c, cnt_y, cnt_z,
    sums, sums_c, half, sums_y, zs, zr, own,
    agz, tmp, hy, cg,
    lb, pay, pay_c, pay_h, pay_y, zs2, zr2,
    blk, agz2, co,
    loc_sem, a2a_s, a2a_r, halo_s, halo_r, ret_s, ret_r, cl_s, cl_r,
):
    NX, NZ, NY, NC, H, T, HD, CH = dims
    NS = NZ * NY * NC
    C = NS
    RPD = T // NX
    HC = C // NC
    ZR = NZ
    HPC = H // CH
    CW = HPC * HD
    WD = H * HD
    scale = HEAD_DIM ** (-0.5)
    s = lax.axis_index("seq")
    x = lax.axis_index("head")
    c = lax.rem(s, NC)
    y = lax.rem(lax.div(s, NC), NY)
    z = lax.div(s, NC * NY)

    def at(zz, yy, cc):
        return ((zz * NY + yy) * NC + cc, x)

    def seq_off(k):
        return (lax.rem(s + k + NS, NS), x)

    def rc(src, dst, ss, rs, dev):
        return pltpu.make_async_remote_copy(
            src_ref=src, dst_ref=dst, send_sem=ss, recv_sem=rs, device_id=dev,
            device_id_type=pl.DeviceIdType.MESH,
        )

    bar = pltpu.get_barrier_semaphore()

    def hello(dev):
        pl.semaphore_signal(bar, inc=1, device_id=dev, device_id_type=pl.DeviceIdType.MESH)

    for d in range(1, NX):
        hello((s, lax.rem(x + d, NX)))
    hello(at(z, y, 1 - c))
    for d in range(1, NY):
        hello(at(z, lax.rem(y + d, NY), c))

    def hello_z(d, carry):
        hello(at(lax.rem(z + d, NZ), y, c))
        return carry

    lax.fori_loop(1, NZ, hello_z, 0)
    for k in (-2, -1, 1, 2):
        hello(seq_off(k))

    row_ids = lax.broadcasted_iota(jnp.int32, (C, C), 0)
    clu_ids = lax.broadcasted_iota(jnp.int32, (C, T), 0)

    def members(h, carry):
        r = slot[pl.ds(h, 1), :]
        ps = lax.rem(r, NC) * (NY * NZ) + lax.rem(lax.div(r, NC), NY) * NZ + lax.div(r, NC * NY)
        slot_pick = jnp.where(ps == row_ids, 1.0, 0.0).astype(BF16)
        clu_pick = jnp.where(clus[pl.ds(h, 1), :] == clu_ids, 1.0, 0.0).astype(BF16)
        m = mm(slot_pick, clu_pick, NN).astype(BF16)
        mem[h] = m
        cnt[0, pl.ds(h, 1), :] = mm(jnp.ones((8, T), BF16), m, NT)[0:1]
        return carry

    lax.fori_loop(0, H, members, 0)
    qi = lax.broadcasted_iota(jnp.int32, (T, 3 * T), 0)
    kj = lax.broadcasted_iota(jnp.int32, (T, 3 * T), 1)
    allowed = (kj <= qi + 2 * T) & (kj > qi + 2 * T - WINDOW_OF(T)) & (kj >= (2 - s) * T)
    bias[...] = jnp.where(allowed, 0.0, -1e30)

    pl.semaphore_wait(bar, (NX - 1) + 1 + (NY - 1) + (NZ - 1) + 4)

    rows_here = pl.ds(pl.multiple_of(x * RPD, RPD), RPD)
    win_here = pl.ds(pl.multiple_of(2 * T + x * RPD, RPD), RPD)
    plan = ((q_in, qb, rows_here), (g_in, gb, rows_here), (k_in, kw, win_here), (v_in, vw, win_here))

    def a2a(i, d):
        src, dst, rows = plan[i]
        to = lax.rem(x + d, NX)
        return rc(
            src.at[:, pl.ds(pl.multiple_of(to * WD, WD), WD)], dst.at[rows, :],
            a2a_s.at[i, d - 1], a2a_r.at[i, d - 1], (s, to),
        )

    def own_copy(i):
        src, dst, rows = plan[i]
        return pltpu.make_async_copy(
            src.at[:, pl.ds(pl.multiple_of(x * WD, WD), WD)], dst.at[rows, :], loc_sem.at[i]
        )

    for i in range(4):
        for d in range(1, NX):
            a2a(i, d).start()
        own_copy(i).start()

    def a2a_wait(i):
        for d in range(1, NX):
            a2a(i, d).wait_recv()
        own_copy(i).wait()

    def c_copy(g, src, dst):
        return rc(src, dst, cl_s.at[g, 0], cl_r.at[g, 0], at(z, y, 1 - c))

    def y_copy(g, d, src, dst):
        return rc(src, dst, cl_s.at[g, d], cl_r.at[g, d], at(z, lax.rem(y + d, NY), c))

    def z_copy(g, d, src, dst):
        return rc(
            src, dst, cl_s.at[g, NY + d - 1], cl_r.at[g, NY + d - 1], at(lax.rem(z + d, NZ), y, c)
        )

    def z_loop(f):
        lax.fori_loop(1, NZ, lambda d, carry: (f(d), carry)[1], 0)

    cc0 = c_copy(0, cnt.at[0], cnt_c)
    cc0.start()
    cc0.wait()
    cnt[1] = cnt[0] + cnt_c[...]
    for d in range(1, NY):
        y_copy(0, d, cnt.at[1], cnt_y.at[d - 1]).start()
    total = cnt[1]
    for d in range(1, NY):
        y_copy(0, d, cnt.at[1], cnt_y.at[d - 1]).wait_recv()
        total = total + cnt_y[d - 1]
    cnt[2] = total
    z_loop(lambda d: z_copy(0, d, cnt.at[2], cnt_z.at[d - 1]).start())

    a2a_wait(0)
    a2a_wait(1)

    def head_cols(h):
        return pl.ds(pl.multiple_of(h * HD, HD), HD)

    def add_sums(h, carry):
        m = mem[h]
        sums[h] = mm(m, qb[:, head_cols(h)], NN)
        sums[H + h] = mm(m, gb[:, head_cols(h)], NN)
        return carry

    lax.fori_loop(0, H, add_sums, 0)
    my_half = pl.ds(pl.multiple_of(c * HC, HC), HC)
    their_half = pl.ds(pl.multiple_of((1 - c) * HC, HC), HC)
    cc1 = c_copy(1, sums.at[:, their_half, :], sums_c)
    cc1.start()
    cc1.wait_recv()

    def add_half(p, carry):
        half[p] = sums[p, my_half, :] + sums_c[p]
        return carry

    lax.fori_loop(0, 2 * H, add_half, 0)

    def y_rows(yy):
        return pl.ds(pl.multiple_of(yy * ZR, ZR), ZR)

    def y1(d):
        return y_copy(1, d, half.at[:, y_rows(lax.rem(y + d, NY)), :], sums_y.at[d - 1])

    for d in range(1, NY):
        y1(d).start()

    def halo(ch, o, kv):
        src = (kw, vw)[kv]
        cols = pl.ds(ch * CW, CW)
        return rc(
            src.at[pl.ds(2 * T, T), cols], src.at[pl.ds((2 - o) * T, T), cols],
            halo_s.at[ch, o - 1, kv], halo_r.at[ch, o - 1, kv], seq_off(o),
        )

    def each_halo(ch, f):
        for o in (2, 1):
            for kv in range(2):
                f(halo(ch, o, kv))

    a2a_wait(2)
    a2a_wait(3)
    each_halo(0, lambda cp: cp.start())

    for d in range(1, NY):
        y1(d).wait_recv()
    for p in range(2 * H):
        v = half[p, y_rows(y), :]
        for d in range(1, NY):
            v = v + sums_y[d - 1, p]
        zs[pl.ds(p, NZ, stride=2 * H), :] = v

    def z1(d):
        to = lax.rem(z + d, NZ)
        rows = pl.ds(pl.multiple_of(to * 2 * H, 2 * H), 2 * H)
        return z_copy(1, d, zs.at[rows, :], zr.at[d - 1])

    z_loop(lambda d: z1(d).start())

    z_loop(lambda d: z_copy(0, d, cnt.at[2], cnt_z.at[d - 1]).wait_recv())
    total = lax.fori_loop(0, NZ - 1, lambda d, t: t + cnt_z[d], cnt[2])
    count = pick(total, c * HC + y * ZR + z)

    z_loop(lambda d: z1(d).wait_recv())
    mine = lax.fori_loop(
        0, NZ - 1, lambda d, t: t + zr[d], zs[pl.ds(pl.multiple_of(z * 2 * H, 2 * H), 2 * H), :]
    )
    centroid = mine[0:H] / count
    cent_out[...] = centroid.astype(BF16)
    own[0:H, :] = centroid
    own[H : 2 * H, :] = mine[H:]
    agz[z] = own[...].astype(BF16)

    def z2(d):
        return z_copy(2, d, agz.at[z], agz.at[z])

    z_loop(lambda d: z2(d).start())
    z_loop(lambda d: z2(d).wait_recv())
    for i in range(NZ):
        tmp[i * 2 * H : (i + 1) * 2 * H, :] = agz[i].astype(F32)
    for p in range(2 * H):
        hy[p] = tmp[pl.ds(p, NZ, stride=2 * H), :].astype(BF16)
    quarter = pl.ds(pl.multiple_of(c * HC + y * ZR, ZR), ZR)

    def y2(d):
        return y_copy(2, d, hy, cg.at[:, quarter, :])

    for d in range(1, NY):
        y2(d).start()
    each_halo(1, lambda cp: cp.start())
    cg[:, quarter, :] = hy[...]
    for d in range(1, NY):
        y2(d).wait_recv()
    cc2 = c_copy(2, cg.at[:, my_half, :], cg.at[:, my_half, :])
    cc2.start()
    cc2.wait_recv()

    lanes_c = lax.broadcasted_iota(jnp.int32, (C, HD), 1)
    pay[H] = jnp.zeros((C, HD), F32)
    pay[H + 1] = jnp.zeros((C, HD), F32)
    own_keys = pl.ds(2 * T, T)

    def logits(h, carry):
        lg = mm(cg[h], kw[own_keys, head_cols(h)], NT) * scale
        lb[h] = lg
        m = jnp.max(lg, axis=1, keepdims=True)
        e = jnp.exp(lg - m)
        pay[h] = mm(e.astype(BF16), vw[own_keys, head_cols(h)], NN)
        pay[H] = jnp.where(lanes_c == h, m, pay[H])
        pay[H + 1] = jnp.where(lanes_c == h, jnp.sum(e, axis=1, keepdims=True), pay[H + 1])
        return carry

    lax.fori_loop(0, H, logits, 0)
    cc3 = c_copy(3, pay.at[:, their_half, :], pay_c)
    cc3.start()

    def window(h, carry):
        cols = head_cols(h)
        q, g = qb[:, cols], gb[:, cols]
        k, v = kw[:, cols], vw[:, cols]
        t = mm(q, k, NT) * scale + bias[...]
        e = jnp.exp(t - jnp.max(t, axis=1, keepdims=True))
        p = e / jnp.sum(e, axis=1, keepdims=True)
        pb = p.astype(BF16)
        wout[:, cols] = mm(pb, v, NN)
        dp = mm(g, v, NT)
        delta = jnp.sum(p * dp, axis=1, keepdims=True)
        ds = (p * (dp - delta) * scale).astype(BF16)
        dq_out[:, cols] = mm(ds, k, NN).astype(BF16)
        part[0, :, cols] = mm(ds, q, TN).astype(BF16)
        part[1, :, cols] = mm(pb, g, TN).astype(BF16)
        return carry

    def back(ch, o):
        cols = pl.ds(ch * CW, CW)
        return rc(
            part.at[:, pl.ds((2 - o) * T, T), cols], ret.at[o - 1, :, :, cols],
            ret_s.at[ch, o - 1], ret_r.at[ch, o - 1], seq_off(-o),
        )

    def do_chunk(ch):
        each_halo(ch, lambda cp: cp.wait_recv())
        lax.fori_loop(ch * HPC, (ch + 1) * HPC, window, 0)
        for o in (2, 1):
            back(ch, o).start()

    cc3.wait_recv()
    ma, mb = pay[H, my_half, :], pay_c[H]
    mm_ = jnp.maximum(ma, mb)
    fa, fb = jnp.exp(ma - mm_), jnp.exp(mb - mm_)
    pay_h[H] = mm_
    pay_h[H + 1] = pay[H + 1, my_half, :] * fa + pay_c[H + 1] * fb
    for h in range(H):
        pay_h[h] = pay[h, my_half, :] * fa[:, h : h + 1] + pay_c[h] * fb[:, h : h + 1]

    def y3(d):
        return y_copy(3, d, pay_h.at[:, y_rows(lax.rem(y + d, NY)), :], pay_y.at[d - 1])

    for d in range(1, NY):
        y3(d).start()

    do_chunk(0)

    for d in range(1, NY):
        y3(d).wait_recv()
    ms = [pay_h[H, y_rows(y), :]] + [pay_y[d, H] for d in range(NY - 1)]
    ls = [pay_h[H + 1, y_rows(y), :]] + [pay_y[d, H + 1] for d in range(NY - 1)]
    top = functools.reduce(jnp.maximum, ms)
    fs = [jnp.exp(m - top) for m in ms]
    for h in range(H):
        v = pay_h[h, y_rows(y), :] * fs[0][:, h : h + 1]
        for d in range(NY - 1):
            v = v + pay_y[d, h] * fs[d + 1][:, h : h + 1]
        zs2[pl.ds(h, NZ, stride=16), :] = v
    zs2[pl.ds(H, NZ, stride=16), :] = top
    zs2[pl.ds(H + 1, NZ, stride=16), :] = functools.reduce(
        lambda a, b: a + b, [a * b for a, b in zip(ls, fs)]
    )
    for p in range(H + 2, 16):
        zs2[pl.ds(p, NZ, stride=16), :] = jnp.zeros((NZ, HD), F32)

    def z3(d):
        to = lax.rem(z + d, NZ)
        rows = pl.ds(pl.multiple_of(to * 16, 16), 16)
        return z_copy(3, d, zs2.at[rows, :], zr2.at[pl.ds(pl.multiple_of(d * 16, 16), 16), :])

    z_loop(lambda d: z3(d).start())
    zr2[0:16, :] = zs2[pl.ds(pl.multiple_of(z * 16, 16), 16), :]

    do_chunk(1)

    z_loop(lambda d: z3(d).wait_recv())
    mz = zr2[pl.ds(H, NZ, stride=16), :]
    lz = zr2[pl.ds(H + 1, NZ, stride=16), :]
    topz = jnp.max(mz, axis=0, keepdims=True)
    fz = jnp.exp(mz - topz)
    lrow = jnp.sum(lz * fz, axis=0, keepdims=True)
    diag = lax.broadcasted_iota(jnp.int32, (H, HD), 0) == lax.broadcasted_iota(
        jnp.int32, (H, HD), 1
    )

    def column(row):
        return jnp.sum(jnp.where(diag, row, 0.0), axis=1, keepdims=True)

    acc = jnp.zeros((H, HD), F32)
    for i in range(NZ):
        acc = acc + zr2[i * 16 : i * 16 + H, :] * column(fz[i : i + 1, :])
    c_out = acc / column(lrow)
    grad = own[H : 2 * H, :].astype(BF16).astype(F32)
    c_delta = jnp.sum(grad * c_out, axis=1, keepdims=True)
    blk[...] = jnp.zeros((16, HD), F32)
    blk[0:H, :] = c_out
    blk[H : H + 1, :] = topz
    blk[H + 1 : H + 2, :] = lrow
    blk[H + 2 : H + 3, :] = jnp.sum(jnp.where(diag, c_delta, 0.0), axis=0, keepdims=True)

    my_rows16 = pl.ds(pl.multiple_of(z * 16, 16), 16)

    def z4(d):
        return z_copy(4, d, blk, agz2.at[my_rows16, :])

    z_loop(lambda d: z4(d).start())
    agz2[my_rows16, :] = blk[...]
    z_loop(lambda d: z4(d).wait_recv())
    for p in range(H + 3):
        co[p, quarter, :] = agz2[pl.ds(p, NZ, stride=16), :]

    def y4(d):
        return y_copy(4, d, co.at[:, quarter, :], co.at[:, quarter, :])

    for d in range(1, NY):
        y4(d).start()
    for d in range(1, NY):
        y4(d).wait_recv()
    cc4 = c_copy(4, co.at[:, my_half, :], co.at[:, my_half, :])
    cc4.start()
    cc4.wait_recv()

    def final(h):
        cols = head_cols(h)
        v = vw[own_keys, cols]
        m, l, delta = pick(co[H], h), pick(co[H + 1], h), pick(co[H + 2], h)
        w = jnp.exp(lb[h] - m) / l
        dw = mm(cg[H + h], v, NT)
        dl = (w * (dw - delta) * scale).astype(BF16)
        out = co[h]
        hi = out.astype(BF16)
        lo = (out - hi.astype(F32)).astype(BF16)
        member = mem[h]
        spread = mm(member, hi, TN) + mm(member, lo, TN)
        attn_out[:, cols] = (wout[:, cols] + spread).astype(BF16)
        dkc = mm(dl, cg[h], TN)
        dvc = mm(w.astype(BF16), cg[H + h], TN)
        for kv, (add, dst) in enumerate(((dkc, dk_out), (dvc, dv_out))):
            t = part[kv, own_keys, cols].astype(F32)
            t = t + ret[0, kv, :, cols].astype(F32) + ret[1, kv, :, cols].astype(F32)
            dst[:, cols] = (t + add).astype(BF16)

    for ch in range(CH):
        for o in (2, 1):
            back(ch, o).wait_recv()
        lax.fori_loop(ch * HPC, (ch + 1) * HPC, lambda h, carry: (final(h), carry)[1], 0)

    for i in range(4):
        for d in range(1, NX):
            a2a(i, d).wait_send()
    for ch in range(CH):
        each_halo(ch, lambda cp: cp.wait_send())
        for o in (2, 1):
            back(ch, o).wait_send()
    for cp in (cc1, cc2, cc3, cc4):
        cp.wait_send()
    for d in range(1, NY):
        y_copy(0, d, cnt.at[1], cnt_y.at[d - 1]).wait_send()
        y1(d).wait_send()
        y2(d).wait_send()
        y3(d).wait_send()
        y4(d).wait_send()

    def drain(d):
        z_copy(0, d, cnt.at[2], cnt_z.at[d - 1]).wait_send()
        z1(d).wait_send()
        z2(d).wait_send()
        z3(d).wait_send()
        z4(d).wait_send()

    z_loop(drain)


def WINDOW_OF(tokens):
    return WINDOW if tokens == 256 else 2 * tokens


def solution(mesh):
    NX = mesh.shape["head"]
    NZ, NY, NC = factors(mesh.shape["seq"])
    HD, CH = HEAD_DIM, 2

    def body(q, k, v, g, clusters, owner_slot):
        H, T = clusters.shape
        C = owner_slot.shape[1]
        WD = H * HD
        HC, ZR = C // NC, NZ
        dims = (NX, NZ, NY, NC, H, T, HD, CH)
        V, D = pltpu.VMEM, pltpu.SemaphoreType.DMA
        groups = 5
        scratch = [
            V((T, WD), BF16), V((T, WD), BF16), V((3 * T, WD), BF16), V((3 * T, WD), BF16),
            V((2, 3 * T, WD), BF16), V((2, 2, T, WD), BF16), V((H, C, T), BF16),
            V((T, WD), F32), V((T, 3 * T), F32),
            V((3, H, C), F32), V((H, C), F32), V((NY - 1, H, C), F32), V((NZ - 1, H, C), F32),
            V((2 * H, C, HD), F32), V((2 * H, HC, HD), F32), V((2 * H, HC, HD), F32),
            V((NY - 1, 2 * H, ZR, HD), F32), V((NZ * 2 * H, HD), F32),
            V((NZ - 1, 2 * H, HD), F32), V((2 * H, HD), F32),
            V((NZ, 2 * H, HD), BF16), V((NZ * 2 * H, HD), F32), V((2 * H, NZ, HD), BF16),
            V((2 * H, C, HD), BF16),
            V((H, C, T), F32), V((H + 2, C, HD), F32), V((H + 2, HC, HD), F32),
            V((H + 2, HC, HD), F32), V((NY - 1, H + 2, ZR, HD), F32),
            V((NZ * 16, HD), F32), V((NZ * 16, HD), F32),
            V((16, HD), F32), V((NZ * 16, HD), F32), V((H + 3, C, HD), F32),
            D((4,)), D((4, NX - 1)), D((4, NX - 1)), D((CH, 2, 2)), D((CH, 2, 2)),
            D((CH, 2)), D((CH, 2)), D((groups, NY + NZ - 1)), D((groups, NY + NZ - 1)),
        ]
        wide = jax.ShapeDtypeStruct((T, WD), BF16)
        hbm = pl.BlockSpec(memory_space=pl.ANY)
        vmem = pl.BlockSpec(memory_space=pltpu.VMEM)
        outs = pl.pallas_call(
            functools.partial(kernel, dims),
            out_shape=(wide, wide, wide, wide, jax.ShapeDtypeStruct((H, HD), BF16)),
            in_specs=[hbm] * 4 + [vmem] * 2,
            out_specs=(vmem,) * 5,
            scratch_shapes=scratch,
            compiler_params=pltpu.CompilerParams(
                collective_id=0, has_side_effects=True, vmem_limit_bytes=60 * 1024 * 1024
            ),
        )(q, k, v, g, clusters, owner_slot)
        return (*outs[:4], outs[4].reshape(H, 1, HD))

    rows = P(("seq", "head"), None)
    return jax.shard_map(
        body,
        mesh=mesh,
        in_specs=(rows, rows, rows, rows, P("head", "seq"), P("head", None)),
        out_specs=(P("seq", "head"),) * 4 + (P("head", "seq", None),),
        check_vma=False,
    )
```

time: 1500 us -> 176 us (0.12)
  the two profiles are of different devices: /device:TPU:1 before, /device:TPU:49 now
where the time goes in v1:
time: 176 us; the launch traced here: 175 us
  Pallas kernels  169 us (96%)
  local copies, waits for them, and re-layouts  5.76 us (3%)
    pallas_call x1, Pallas kernels, body(): pl.pallas_call(functools.partial(kernel, dims), out_shape=(wide, wide, wi...  169 us
    unnamed x13, local copies, waits for them, and re-layouts  5.76 us

profile of v1, /device:TPU:49, one launch (start us, length us, event | category | flops | bytes accessed | tf_op | source)
XLA Modules:
  0.0 175.4 jit_solution(14857938629224663544)
XLA Ops:
  0.6 169.0 %shard_map.101 = (bf16[256,1024]{1,0:T(8,128)(2,1)}, bf16[256,1024]{1,0:T(8,128)(2,1)}, bf16[256,1024]{1,0:T(8,128)(2,1)}, bf16[256,1024]{1,0:T(8,128)(2,1)}, bf16[8,128]{1,0:T(8,128)(2,1)}) custom-call(bf16[64,4096]{1,0:T(8,128)(2,1)} %q_in.1, bf16[64,4096]{1,0:T(8,128)(2,1)} %k_in.1, bf16[64,4096]{1,0:T(8,128)(2,1)} %v_in.1, bf16[64,4096]{1,0:T(8,128)(2,1)} %g_in.1, ...), custom_call_target="tpu_custom_call" | custom-call | tf_op jit(solution)/shard_map/pallas_call | solution.py:498
  169.6 0.0 copy-start.2
  169.7 1.9 %copy.16 = bf16[256,1024]{1,0:T(8,128)(2,1)} copy(bf16[256,1024]{1,0:T(8,128)(2,1)} %get-tuple-element.20) | data formatting | bytes 1048576
  171.6 0.0 copy-done.2
  171.6 0.0 copy-start.1
  171.6 0.8 copy.17
  172.4 0.4 copy-done.1
  172.8 0.0 copy-start
  172.8 0.8 copy.18
  173.6 0.4 copy-done
  174.0 0.0 copy-start.3
  174.0 0.8 copy.19
  174.8 0.0 copy-done.3
  174.8 0.6 copy.20
Async XLA Ops:
  169.6 1.9 %copy-start.2 = (bf16[256,1024]{1,0:T(8,128)(2,1)S(1)}, bf16[256,1024]{1,0:T(8,128)(2,1)}, u32[]{:S(2)}) copy-start(bf16[256,1024]{1,0:T(8,128)(2,1)} %get-tuple-element.21) | copy-start | bytes 1572868
  171.6 1.2 copy-start.1
  172.8 1.2 copy-start
  174.0 0.8 copy-start.3

commit v2 on v1

v2 whole, which is shorter than its diff:
```python
import functools

import jax
import jax.numpy as jnp
from jax import lax
from jax.experimental import pallas as pl
from jax.experimental.pallas import tpu as pltpu
from jax.sharding import PartitionSpec as P

HEAD_DIM = 128
WINDOW = 512
F32 = jnp.float32
BF16 = jnp.bfloat16
NN = (((1,), (0,)), ((), ()))
NT = (((1,), (1,)), ((), ()))
TN = (((0,), (0,)), ((), ()))


def factors(count):
    return {128: (16, 4, 2), 8: (2, 2, 2)}[count]


def mm(a, b, dims):
    return lax.dot_general(a, b, dims, preferred_element_type=F32)


def split(v):
    hi = v.astype(BF16)
    rest = v - hi.astype(F32)
    mid = rest.astype(BF16)
    return hi, mid, (rest - mid.astype(F32)).astype(BF16)


def join(parts):
    return functools.reduce(lambda a, b: a + b, [p.astype(F32) for p in parts])


def pick(table, lane):
    lanes = lax.broadcasted_iota(jnp.int32, table.shape, 1)
    return jnp.sum(jnp.where(lanes == lane, table, 0.0), axis=1, keepdims=True)


def kernel(
    dims, q_in, k_in, v_in, g_in, clus, slot, attn_out, dq_out, dk_out, dv_out, cent_out,
    qw, gw, kw, vw, dkw, dvw, mem, wout, bias, bias_t, sta, st,
    cnt, cnt_c, cnt_y, cnt_z,
    sums, sums_c, half, half_b, sums_y, zs, zb, zr, own,
    agz, tmp, hy, cg,
    lb, pay, pay_c, pay_h, pay_b, pay_y, zs2, zb2, zr2,
    blk, agz2, co,
    loc_sem, a2a_s, a2a_r, far_s, far_r, near_s, near_r, st_s, st_r, cl_s, cl_r,
):
    NX, NZ, NY, NC, H, T, HD, CH = dims
    NS = NZ * NY * NC
    C = NS
    RPD = T // NX
    HC = C // NC
    ZR = NZ
    HPC = H // CH
    CW = HPC * HD
    WD = H * HD
    scale = HEAD_DIM ** (-0.5)
    s = lax.axis_index("seq")
    x = lax.axis_index("head")
    c = lax.rem(s, NC)
    y = lax.rem(lax.div(s, NC), NY)
    z = lax.div(s, NC * NY)

    def at(zz, yy, cc):
        return ((zz * NY + yy) * NC + cc, x)

    def seq_off(k):
        return (lax.rem(s + k + NS, NS), x)

    def rc(src, dst, ss, rs, dev):
        return pltpu.make_async_remote_copy(
            src_ref=src, dst_ref=dst, send_sem=ss, recv_sem=rs, device_id=dev,
            device_id_type=pl.DeviceIdType.MESH,
        )

    bar = pltpu.get_barrier_semaphore()

    def hello(dev):
        pl.semaphore_signal(bar, inc=1, device_id=dev, device_id_type=pl.DeviceIdType.MESH)

    for d in range(1, NX):
        hello((s, lax.rem(x + d, NX)))
    hello(at(z, y, 1 - c))
    for d in range(1, NY):
        hello(at(z, lax.rem(y + d, NY), c))

    def hello_z(d, carry):
        hello(at(lax.rem(z + d, NZ), y, c))
        return carry

    lax.fori_loop(1, NZ, hello_z, 0)
    for k in (-2, -1, 1, 2):
        hello(seq_off(k))

    row_ids = lax.broadcasted_iota(jnp.int32, (C, C), 0)
    clu_ids = lax.broadcasted_iota(jnp.int32, (C, T), 0)

    def members(h, carry):
        r = slot[pl.ds(h, 1), :]
        ps = lax.rem(r, NC) * (NY * NZ) + lax.rem(lax.div(r, NC), NY) * NZ + lax.div(r, NC * NY)
        slot_pick = jnp.where(ps == row_ids, 1.0, 0.0).astype(BF16)
        clu_pick = jnp.where(clus[pl.ds(h, 1), :] == clu_ids, 1.0, 0.0).astype(BF16)
        m = mm(slot_pick, clu_pick, NN).astype(BF16)
        mem[h] = m
        cnt[0, pl.ds(h, 1), :] = mm(jnp.ones((8, T), BF16), m, NT)[0:1]
        return carry

    lax.fori_loop(0, H, members, 0)
    qi = lax.broadcasted_iota(jnp.int32, (T, 3 * T), 0)
    kj = lax.broadcasted_iota(jnp.int32, (T, 3 * T), 1)
    allowed = (kj <= qi + 2 * T) & (kj > qi + 2 * T - WINDOW_OF(T)) & (kj >= (2 - s) * T)
    bias[...] = jnp.where(allowed, 0.0, -1e30)
    allowed = (qi <= kj) & (qi > kj - WINDOW_OF(T)) & (kj < (NS - s) * T)
    bias_t[...] = jnp.where(allowed, 0.0, -1e30)

    pl.semaphore_wait(bar, (NX - 1) + 1 + (NY - 1) + (NZ - 1) + 4)

    plan = ((k_in, kw, 2 * T), (v_in, vw, 2 * T), (q_in, qw, 0), (g_in, gw, 0))

    def a2a_slices(i, ch, to):
        src, dst, first = plan[i]
        return (
            src.at[:, pl.ds(pl.multiple_of(to * WD + ch * CW, CW), CW)],
            dst.at[pl.ds(pl.multiple_of(first + x * RPD, RPD), RPD), pl.ds(ch * CW, CW)],
        )

    def a2a(i, ch, d):
        to = lax.rem(x + d, NX)
        return rc(*a2a_slices(i, ch, to), a2a_s.at[i, ch, d - 1], a2a_r.at[i, ch, d - 1], (s, to))

    def own_copy(i, ch):
        return pltpu.make_async_copy(*a2a_slices(i, ch, x), loc_sem.at[i, ch])

    for ch in range(CH):
        for i in range(4):
            for d in range(1, NX):
                a2a(i, ch, d).start()
            own_copy(i, ch).start()

    def a2a_wait(ch):
        for i in range(4):
            for d in range(1, NX):
                a2a(i, ch, d).wait_recv()
            own_copy(i, ch).wait()

    def far(i, ch):
        buf, first = plan[i][1], plan[i][2]
        cols = pl.ds(ch * CW, CW)
        return rc(
            buf.at[pl.ds(first, T), cols], buf.at[pl.ds(2 * T - first, T), cols],
            far_s.at[i, ch], far_r.at[i, ch], seq_off(2 if i < 2 else -2),
        )

    def near(i, ch):
        buf = plan[i][1]
        cols = pl.ds(ch * CW, CW)
        first = 2 * T * (1 - c)
        return rc(
            buf.at[pl.ds(pl.multiple_of(first, T), T), cols], buf.at[pl.ds(T, T), cols],
            near_s.at[i, ch], near_r.at[i, ch], at(z, y, 1 - c),
        )

    def send_near(ch, core, pair):
        @pl.when(c == core)
        def _():
            for i in pair:
                near(i, ch).start()

    def halo_start(ch):
        for i in range(4):
            far(i, ch).start()
        send_near(ch, 0, (0, 1))
        send_near(ch, 1, (2, 3))

    def halo_pass(ch):
        for i in range(4):
            far(i, ch).wait_recv()
        send_near(ch, 1, (0, 1))
        send_near(ch, 0, (2, 3))

    def c_copy(g, src, dst):
        return rc(src, dst, cl_s.at[g, 0], cl_r.at[g, 0], at(z, y, 1 - c))

    def y_copy(g, d, src, dst):
        return rc(src, dst, cl_s.at[g, d], cl_r.at[g, d], at(z, lax.rem(y + d, NY), c))

    def z_copy(g, d, src, dst):
        return rc(
            src, dst, cl_s.at[g, NY + d - 1], cl_r.at[g, NY + d - 1], at(lax.rem(z + d, NZ), y, c)
        )

    def z_loop(f):
        lax.fori_loop(1, NZ, lambda d, carry: (f(d), carry)[1], 0)

    cc0 = c_copy(0, cnt.at[0], cnt_c)
    cc0.start()
    cc0.wait()
    cnt[1] = cnt[0] + cnt_c[...]
    for d in range(1, NY):
        y_copy(0, d, cnt.at[1], cnt_y.at[d - 1]).start()
    total = cnt[1]
    for d in range(1, NY):
        y_copy(0, d, cnt.at[1], cnt_y.at[d - 1]).wait_recv()
        total = total + cnt_y[d - 1]
    cnt[2] = total
    z_loop(lambda d: z_copy(0, d, cnt.at[2], cnt_z.at[d - 1]).start())

    def head_cols(h):
        return pl.ds(pl.multiple_of(h * HD, HD), HD)

    own_rows = pl.ds(0, T)

    def add_sums(h, carry):
        m = mem[h]
        sums[h] = mm(m, qw[own_rows, head_cols(h)], NN)
        sums[H + h] = mm(m, gw[own_rows, head_cols(h)], NN)
        return carry

    for ch in range(CH):
        a2a_wait(ch)
        halo_start(ch)
        lax.fori_loop(ch * HPC, (ch + 1) * HPC, add_sums, 0)
        if ch > 1:
            halo_pass(ch - 2)
    my_half = pl.ds(pl.multiple_of(c * HC, HC), HC)
    their_half = pl.ds(pl.multiple_of((1 - c) * HC, HC), HC)
    cc1 = c_copy(1, sums.at[:, their_half, :], sums_c)
    cc1.start()
    cc1.wait_recv()

    def add_half(p, carry):
        v = sums[p, my_half, :] + sums_c[p]
        half[p] = v
        half_b[p] = v.astype(BF16)
        return carry

    lax.fori_loop(0, 2 * H, add_half, 0)

    def y_rows(yy):
        return pl.ds(pl.multiple_of(yy * ZR, ZR), ZR)

    def y1(d):
        return y_copy(1, d, half_b.at[:, y_rows(lax.rem(y + d, NY)), :], sums_y.at[d - 1])

    for d in range(1, NY):
        y1(d).start()

    for ch in range(max(CH - 2, 0), CH):
        halo_pass(ch)
    for d in range(1, NY):
        y1(d).wait_recv()
    for p in range(2 * H):
        v = half[p, y_rows(y), :]
        for d in range(1, NY):
            v = v + sums_y[d - 1, p].astype(F32)
        zs[pl.ds(p, NZ, stride=2 * H), :] = v

    def z1(d):
        to = lax.rem(z + d, NZ)
        rows = pl.ds(pl.multiple_of(to * 2 * H, 2 * H), 2 * H)
        return z_copy(1, d, zb.at[rows, :], zr.at[d - 1])

    zb[...] = zs[...].astype(BF16)
    z_loop(lambda d: z1(d).start())

    own_keys = pl.ds(2 * T, T)
    lanes_t = lax.broadcasted_iota(jnp.int32, (T, HD), 1)

    def query_side(h, carry):
        cols = head_cols(h)
        k, v = kw[:, cols], vw[:, cols]
        t = mm(qw[own_rows, cols], k, NT) * scale + bias[...]
        m = jnp.max(t, axis=1, keepdims=True)
        e = jnp.exp(t - m)
        rl = 1.0 / jnp.sum(e, axis=1, keepdims=True)
        p = e * rl
        wout[:, cols] = mm(p.astype(BF16), v, NN)
        dp = mm(gw[own_rows, cols], v, NT)
        delta = jnp.sum(p * dp, axis=1, keepdims=True)
        ds = (p * (dp - delta) * scale).astype(BF16)
        dq_out[:, cols] = mm(ds, k, NN).astype(BF16)
        old = jnp.where(lanes_t == h, m, sta[...])
        old = jnp.where(lanes_t == H + h, rl, old)
        sta[...] = jnp.where(lanes_t == 2 * H + h, delta, old)
        return carry

    def key_side(h, carry):
        cols = head_cols(h)
        q, g = qw[:, cols], gw[:, cols]
        t = mm(kw[own_keys, cols], q, NT) * scale + bias_t[...]
        p = jnp.exp(t - st[pl.ds(h, 1), :]) * st[pl.ds(H + h, 1), :]
        dp = mm(vw[own_keys, cols], g, NT)
        ds = (p * (dp - st[pl.ds(2 * H + h, 1), :]) * scale).astype(BF16)
        dkw[:, cols] = mm(ds, q, NN)
        dvw[:, cols] = mm(p.astype(BF16), g, NN)
        return carry

    def stat(o):
        return rc(
            st.at[:, pl.ds(0, T)], st.at[:, pl.ds(o * T, T)], st_s.at[o - 1], st_r.at[o - 1], seq_off(-o)
        )

    for ch in range(CH):
        for i in range(4):
            near(i, ch).wait_recv()

    sta[...] = jnp.zeros((T, HD), F32)
    early = H * 5 // 8
    lax.fori_loop(0, early, query_side, 0)
    z_loop(lambda d: z_copy(0, d, cnt.at[2], cnt_z.at[d - 1]).wait_recv())
    total = lax.fori_loop(0, NZ - 1, lambda d, t: t + cnt_z[d], cnt[2])
    count = pick(total, c * HC + y * ZR + z)

    z_loop(lambda d: z1(d).wait_recv())
    mine = lax.fori_loop(
        0, NZ - 1, lambda d, t: t + zr[d].astype(F32), zs[pl.ds(pl.multiple_of(z * 2 * H, 2 * H), 2 * H), :]
    )
    centroid = mine[0:H] / count
    cent_out[...] = centroid.astype(BF16)
    own[0:H, :] = centroid
    own[H : 2 * H, :] = mine[H:]
    agz[z] = own[...].astype(BF16)

    def z2(d):
        return z_copy(2, d, agz.at[z], agz.at[z])

    z_loop(lambda d: z2(d).start())
    lax.fori_loop(early, H, query_side, 0)
    st[:, 0:T] = jnp.transpose(sta[...])[0 : 3 * H]
    for o in (1, 2):
        stat(o).start()

    z_loop(lambda d: z2(d).wait_recv())
    for i in range(NZ):
        tmp[i * 2 * H : (i + 1) * 2 * H, :] = agz[i].astype(F32)
    for p in range(2 * H):
        hy[p] = tmp[pl.ds(p, NZ, stride=2 * H), :].astype(BF16)
    quarter = pl.ds(pl.multiple_of(c * HC + y * ZR, ZR), ZR)

    def y2(d):
        return y_copy(2, d, hy, cg.at[:, quarter, :])

    for d in range(1, NY):
        y2(d).start()
    cg[:, quarter, :] = hy[...]
    for d in range(1, NY):
        y2(d).wait_recv()
    cc2 = c_copy(2, cg.at[:, my_half, :], cg.at[:, my_half, :])
    cc2.start()
    cc2.wait_recv()

    lanes_c = lax.broadcasted_iota(jnp.int32, (C, HD), 1)
    tops, masses = jnp.zeros((C, HD), F32), jnp.zeros((C, HD), F32)
    for h in range(H):
        lg = mm(cg[h], kw[own_keys, head_cols(h)], NT) * scale
        lb[h] = lg
        m = jnp.max(lg, axis=1, keepdims=True)
        e = jnp.exp(lg - m)
        pay[h] = mm(e.astype(BF16), vw[own_keys, head_cols(h)], NN)
        tops = jnp.where(lanes_c == h, m, tops)
        masses = jnp.where(lanes_c == h, jnp.sum(e, axis=1, keepdims=True), masses)
    pay[H] = tops
    pay[H + 1] = masses
    cc3 = c_copy(3, pay.at[:, their_half, :], pay_c)
    cc3.start()

    cc3.wait_recv()
    ma, mb = pay[H, my_half, :], pay_c[H]
    mm_ = jnp.maximum(ma, mb)
    fa, fb = jnp.exp(ma - mm_), jnp.exp(mb - mm_)
    mass = pay[H + 1, my_half, :] * fa + pay_c[H + 1] * fb
    pay_h[H] = mm_
    pay_h[H + 1] = mass
    for n, v in enumerate(split(mm_) + split(mass)):
        pay_b[H + n] = v
    for h in range(H):
        v = pay[h, my_half, :] * fa[:, h : h + 1] + pay_c[h] * fb[:, h : h + 1]
        pay_h[h] = v
        pay_b[h] = v.astype(BF16)

    def y3(d):
        return y_copy(3, d, pay_b.at[:, y_rows(lax.rem(y + d, NY)), :], pay_y.at[d - 1])

    for d in range(1, NY):
        y3(d).start()

    for d in range(1, NY):
        y3(d).wait_recv()
    ms = [pay_h[H, y_rows(y), :]] + [join([pay_y[d, H + n] for n in range(3)]) for d in range(NY - 1)]
    ls = [pay_h[H + 1, y_rows(y), :]] + [
        join([pay_y[d, H + 3 + n] for n in range(3)]) for d in range(NY - 1)
    ]
    top = functools.reduce(jnp.maximum, ms)
    fs = [jnp.exp(m - top) for m in ms]
    for h in range(H):
        v = pay_h[h, y_rows(y), :] * fs[0][:, h : h + 1]
        for d in range(NY - 1):
            v = v + pay_y[d, h].astype(F32) * fs[d + 1][:, h : h + 1]
        zs2[pl.ds(h, NZ, stride=16), :] = v
    mass = functools.reduce(lambda a, b: a + b, [a * b for a, b in zip(ls, fs)])
    for n, v in enumerate(split(top) + split(mass)):
        zs2[pl.ds(H + n, NZ, stride=16), :] = v.astype(F32)
    for p in range(H + 6, 16):
        zs2[pl.ds(p, NZ, stride=16), :] = jnp.zeros((NZ, HD), F32)
    zb2[...] = zs2[...].astype(BF16)

    def z3(d):
        to = lax.rem(z + d, NZ)
        rows = pl.ds(pl.multiple_of(to * 16, 16), 16)
        return z_copy(3, d, zb2.at[rows, :], zr2.at[pl.ds(pl.multiple_of(d * 16, 16), 16), :])

    z_loop(lambda d: z3(d).start())
    zr2[0:16, :] = zb2[pl.ds(pl.multiple_of(z * 16, 16), 16), :]

    for o in (1, 2):
        stat(o).wait_recv()
    lax.fori_loop(0, H, key_side, 0)
    z_loop(lambda d: z3(d).wait_recv())
    tmp[0 : NZ * 16, :] = zr2[...].astype(F32)
    mz = join([tmp[pl.ds(H + n, NZ, stride=16), :] for n in range(3)])
    lz = join([tmp[pl.ds(H + 3 + n, NZ, stride=16), :] for n in range(3)])
    topz = jnp.max(mz, axis=0, keepdims=True)
    fz = jnp.exp(mz - topz)
    lrow = jnp.sum(lz * fz, axis=0, keepdims=True)
    diag = lax.broadcasted_iota(jnp.int32, (H, HD), 0) == lax.broadcasted_iota(
        jnp.int32, (H, HD), 1
    )

    def column(row):
        return jnp.sum(jnp.where(diag, row, 0.0), axis=1, keepdims=True)

    acc = jnp.zeros((H, HD), F32)
    for i in range(NZ):
        acc = acc + tmp[i * 16 : i * 16 + H, :] * column(fz[i : i + 1, :])
    c_out = acc / column(lrow)
    grad = own[H : 2 * H, :].astype(BF16).astype(F32)
    c_delta = jnp.sum(grad * c_out, axis=1, keepdims=True)
    tmp[0:16, :] = jnp.zeros((16, HD), F32)
    tmp[0:H, :] = c_out
    delta_row = jnp.sum(jnp.where(diag, c_delta, 0.0), axis=0, keepdims=True)
    for n, v in enumerate(split(topz + jnp.log(jnp.where(lrow > 0.0, lrow, 1.0))) + split(delta_row)):
        tmp[H + n : H + n + 1, :] = v.astype(F32)
    blk[...] = tmp[0:16, :].astype(BF16)

    my_rows16 = pl.ds(pl.multiple_of(z * 16, 16), 16)

    def z4(d):
        return z_copy(4, d, blk, agz2.at[my_rows16, :])

    z_loop(lambda d: z4(d).start())
    agz2[my_rows16, :] = blk[...]
    z_loop(lambda d: z4(d).wait_recv())
    tmp[0 : NZ * 16, :] = agz2[...].astype(F32)
    for p in range(H + 6):
        co[p, quarter, :] = tmp[pl.ds(p, NZ, stride=16), :].astype(BF16)

    def y4(d):
        return y_copy(4, d, co.at[:, quarter, :], co.at[:, quarter, :])

    for d in range(1, NY):
        y4(d).start()
    for d in range(1, NY):
        y4(d).wait_recv()
    cc4 = c_copy(4, co.at[:, my_half, :], co.at[:, my_half, :])
    cc4.start()
    cc4.wait_recv()

    lse = join([co[H + n] for n in range(3)])
    deltas = join([co[H + 3 + n] for n in range(3)])
    for h in range(H):
        cols = head_cols(h)
        w = jnp.exp(lb[h] - pick(lse, h))
        dw = mm(cg[H + h], vw[own_keys, cols], NT)
        dl = (w * (dw - pick(deltas, h)) * scale).astype(BF16)
        attn_out[:, cols] = (wout[:, cols] + mm(mem[h], co[h], TN)).astype(BF16)
        dk_out[:, cols] = (dkw[:, cols] + mm(dl, cg[h], TN)).astype(BF16)
        dv_out[:, cols] = (dvw[:, cols] + mm(w.astype(BF16), cg[H + h], TN)).astype(BF16)

    for ch in range(CH):
        for i in range(4):
            for d in range(1, NX):
                a2a(i, ch, d).wait_send()
            far(i, ch).wait_send()
            near(i, ch).wait_send()
    for o in (1, 2):
        stat(o).wait_send()
    for cp in (cc1, cc2, cc3, cc4):
        cp.wait_send()
    for d in range(1, NY):
        y_copy(0, d, cnt.at[1], cnt_y.at[d - 1]).wait_send()
        y1(d).wait_send()
        y2(d).wait_send()
        y3(d).wait_send()
        y4(d).wait_send()

    def drain(d):
        z_copy(0, d, cnt.at[2], cnt_z.at[d - 1]).wait_send()
        z1(d).wait_send()
        z2(d).wait_send()
        z3(d).wait_send()
        z4(d).wait_send()

    z_loop(drain)


def WINDOW_OF(tokens):
    return WINDOW if tokens == 256 else 2 * tokens


def solution(mesh):
    NX = mesh.shape["head"]
    NZ, NY, NC = factors(mesh.shape["seq"])
    HD, CH = HEAD_DIM, 4

    def body(q, k, v, g, clusters, owner_slot):
        H, T = clusters.shape
        C = owner_slot.shape[1]
        WD = H * HD
        HC, ZR = C // NC, NZ
        dims = (NX, NZ, NY, NC, H, T, HD, CH)
        V, D = pltpu.VMEM, pltpu.SemaphoreType.DMA
        groups = 5
        scratch = [
            V((3 * T, WD), BF16), V((3 * T, WD), BF16), V((3 * T, WD), BF16), V((3 * T, WD), BF16),
            V((T, WD), F32), V((T, WD), F32), V((H, C, T), BF16),
            V((T, WD), F32), V((T, 3 * T), F32), V((T, 3 * T), F32), V((T, HD), F32),
            V((3 * H, 3 * T), F32),
            V((3, H, C), F32), V((H, C), F32), V((NY - 1, H, C), F32), V((NZ - 1, H, C), F32),
            V((2 * H, C, HD), F32), V((2 * H, HC, HD), F32), V((2 * H, HC, HD), F32),
            V((2 * H, HC, HD), BF16), V((NY - 1, 2 * H, ZR, HD), BF16), V((NZ * 2 * H, HD), F32),
            V((NZ * 2 * H, HD), BF16), V((NZ - 1, 2 * H, HD), BF16), V((2 * H, HD), F32),
            V((NZ, 2 * H, HD), BF16), V((NZ * 16, HD), F32), V((2 * H, NZ, HD), BF16),
            V((2 * H, C, HD), BF16),
            V((H, C, T), F32), V((H + 2, C, HD), F32), V((H + 2, HC, HD), F32),
            V((H + 2, HC, HD), F32), V((H + 6, HC, HD), BF16), V((NY - 1, H + 6, ZR, HD), BF16),
            V((NZ * 16, HD), F32), V((NZ * 16, HD), BF16), V((NZ * 16, HD), BF16),
            V((16, HD), BF16), V((NZ * 16, HD), BF16), V((H + 6, C, HD), BF16),
            D((4, CH)), D((4, CH, NX - 1)), D((4, CH, NX - 1)), D((4, CH)), D((4, CH)),
            D((4, CH)), D((4, CH)), D((2,)), D((2,)), D((groups, NY + NZ - 1)), D((groups, NY + NZ - 1)),
        ]
        wide = jax.ShapeDtypeStruct((T, WD), BF16)
        hbm = pl.BlockSpec(memory_space=pl.ANY)
        vmem = pl.BlockSpec(memory_space=pltpu.VMEM)
        outs = pl.pallas_call(
            functools.partial(kernel, dims),
            out_shape=(wide, wide, wide, wide, jax.ShapeDtypeStruct((H, HD), BF16)),
            in_specs=[hbm] * 4 + [vmem] * 2,
            out_specs=(vmem,) * 5,
            scratch_shapes=scratch,
            compiler_params=pltpu.CompilerParams(
                collective_id=0, has_side_effects=True, vmem_limit_bytes=60 * 1024 * 1024
            ),
        )(q, k, v, g, clusters, owner_slot)
        return (*outs[:4], outs[4].reshape(H, 1, HD))

    rows = P(("seq", "head"), None)
    return jax.shard_map(
        body,
        mesh=mesh,
        in_specs=(rows, rows, rows, rows, P("head", "seq"), P("head", None)),
        out_specs=(P("seq", "head"),) * 4 + (P("head", "seq", None),),
        check_vma=False,
    )
```

time: 176 us -> 118 us (0.67)
  the two profiles are of different devices: /device:TPU:49 before, /device:TPU:1 now
where the time goes in v2:
time: 118 us
  Pallas kernels  112 us (95%)
  local copies, waits for them, and re-layouts  5.76 us (5%)
    pallas_call x1, Pallas kernels, body(): pl.pallas_call(functools.partial(kernel, dims), out_shape=(wide, wide, wi...  112 us
    unnamed x13, local copies, waits for them, and re-layouts  5.76 us

profile of v2, /device:TPU:1, one launch (start us, length us, event | category | flops | bytes accessed | tf_op | source)
XLA Modules:
  0.0 118.0 jit_solution(12157654848344042511)
XLA Ops:
  0.6 111.6 %shard_map.101 = (bf16[256,1024]{1,0:T(8,128)(2,1)}, bf16[256,1024]{1,0:T(8,128)(2,1)}, bf16[256,1024]{1,0:T(8,128)(2,1)}, bf16[256,1024]{1,0:T(8,128)(2,1)}, bf16[8,128]{1,0:T(8,128)(2,1)}) custom-call(bf16[64,4096]{1,0:T(8,128)(2,1)} %q_in.1, bf16[64,4096]{1,0:T(8,128)(2,1)} %k_in.1, bf16[64,4096]{1,0:T(8,128)(2,1)} %v_in.1, bf16[64,4096]{1,0:T(8,128)(2,1)} %g_in.1, ...), custom_call_target="tpu_custom_call" | custom-call | tf_op jit(solution)/shard_map/pallas_call | solution.py:549
  112.2 0.0 copy-start.2
  112.2 1.9 %copy.16 = bf16[256,1024]{1,0:T(8,128)(2,1)} copy(bf16[256,1024]{1,0:T(8,128)(2,1)} %get-tuple-element.20) | data formatting | bytes 1048576
  114.2 0.0 copy-done.2
  114.2 0.0 copy-start.1
  114.2 0.8 copy.17
  115.0 0.4 copy-done.1
  115.4 0.0 copy-start
  115.4 0.8 copy.18
  116.2 0.4 copy-done
  116.6 0.0 copy-start.3
  116.6 0.8 copy.19
  117.4 0.0 copy-done.3
  117.4 0.6 copy.20
Async XLA Ops:
  112.2 1.9 %copy-start.2 = (bf16[256,1024]{1,0:T(8,128)(2,1)S(1)}, bf16[256,1024]{1,0:T(8,128)(2,1)}, u32[]{:S(2)}) copy-start(bf16[256,1024]{1,0:T(8,128)(2,1)} %get-tuple-element.21) | copy-start | bytes 1572868
  114.2 1.2 %copy-start.1 = (bf16[256,1024]{1,0:T(8,128)(2,1)S(1)}, bf16[256,1024]{1,0:T(8,128)(2,1)}, u32[]{:S(2)}) copy-start(bf16[256,1024]{1,0:T(8,128)(2,1)} %get-tuple-element.22) | copy-start | bytes 1572868
  115.4 1.2 %copy-start = (bf16[256,1024]{1,0:T(8,128)(2,1)S(1)}, bf16[256,1024]{1,0:T(8,128)(2,1)}, u32[]{:S(2)}) copy-start(bf16[256,1024]{1,0:T(8,128)(2,1)} %get-tuple-element.23) | copy-start | bytes 1572868
  116.6 0.8 copy-start.3

commit v3 on v2

--- a/solution.py
+++ b/solution.py
@@ -41,14 +41,14 @@
 
 
 def kernel(
-    dims, q_in, k_in, v_in, g_in, clus, slot, attn_out, dq_out, dk_out, dv_out, cent_out,
+    dims, q_in, k_in, v_in, g_in, clus_in, slot_in, attn_out, dq_out, dk_out, dv_out, cent_out,
     qw, gw, kw, vw, dkw, dvw, mem, wout, bias, bias_t, sta, st,
     cnt, cnt_c, cnt_y, cnt_z,
     sums, sums_c, half, half_b, sums_y, zs, zb, zr, own,
     agz, tmp, hy, cg,
     lb, pay, pay_c, pay_h, pay_b, pay_y, zs2, zb2, zr2,
-    blk, agz2, co,
-    loc_sem, a2a_s, a2a_r, far_s, far_r, near_s, near_r, st_s, st_r, cl_s, cl_r,
+    blk, agz2, co, clus, slot,
+    loc_sem, a2a_s, a2a_r, far_s, far_r, near_s, near_r, st_s, st_r, cl_s, cl_r, co_s, co_r, ids_sem,
 ):
     NX, NZ, NY, NC, H, T, HD, CH = dims
     NS = NZ * NY * NC
@@ -78,6 +78,12 @@
             device_id_type=pl.DeviceIdType.MESH,
         )
 
+    ids = (
+        pltpu.make_async_copy(clus_in, clus, ids_sem.at[0]),
+        pltpu.make_async_copy(slot_in, slot, ids_sem.at[1]),
+    )
+    for cp in ids:
+        cp.start()
     bar = pltpu.get_barrier_semaphore()
 
     def hello(dev):
@@ -97,6 +103,73 @@
     for k in (-2, -1, 1, 2):
         hello(seq_off(k))
 
+    pl.semaphore_wait(bar, (NX - 1) + 1 + (NY - 1) + (NZ - 1) + 4)
+
+    plan = ((k_in, kw, 2 * T), (v_in, vw, 2 * T), (q_in, qw, 0), (g_in, gw, 0))
+
+    def a2a_slices(i, ch, to):
+        src, dst, first = plan[i]
+        return (
+            src.at[:, pl.ds(pl.multiple_of(to * WD + ch * CW, CW), CW)],
+            dst.at[pl.ds(pl.multiple_of(first + x * RPD, RPD), RPD), pl.ds(ch * CW, CW)],
+        )
+
+    def a2a(i, ch, d):
+        to = lax.rem(x + d, NX)
+        return rc(*a2a_slices(i, ch, to), a2a_s.at[i, ch, d - 1], a2a_r.at[i, ch, d - 1], (s, to))
+
+    def own_copy(i, ch):
+        return pltpu.make_async_copy(*a2a_slices(i, ch, x), loc_sem.at[i, ch])
+
+    for ch in range(CH):
+        for i in range(4):
+            for d in range(1, NX):
+                a2a(i, ch, d).start()
+            own_copy(i, ch).start()
+
+    def a2a_wait(ch):
+        for i in range(4):
+            for d in range(1, NX):
+                a2a(i, ch, d).wait_recv()
+            own_copy(i, ch).wait()
+
+    def far(i, ch):
+        buf, first = plan[i][1], plan[i][2]
+        cols = pl.ds(ch * CW, CW)
+        return rc(
+            buf.at[pl.ds(first, T), cols], buf.at[pl.ds(2 * T - first, T), cols],
+            far_s.at[i, ch], far_r.at[i, ch], seq_off(2 if i < 2 else -2),
+        )
+
+    def near(i, ch):
+        buf = plan[i][1]
+        cols = pl.ds(ch * CW, CW)
+        first = 2 * T * (1 - c)
+        return rc(
+            buf.at[pl.ds(pl.multiple_of(first, T), T), cols], buf.at[pl.ds(T, T), cols],
+            near_s.at[i, ch], near_r.at[i, ch], at(z, y, 1 - c),
+        )
+
+    def send_near(ch, core, pair):
+        @pl.when(c == core)
+        def _():
+            for i in pair:
+                near(i, ch).start()
+
+    def halo_start(ch):
+        for i in range(4):
+            far(i, ch).start()
+        send_near(ch, 0, (0, 1))
+        send_near(ch, 1, (2, 3))
+
+    def halo_pass(ch):
+        for i in range(4):
+            far(i, ch).wait_recv()
+        send_near(ch, 1, (0, 1))
+        send_near(ch, 0, (2, 3))
+
+    for cp in ids:
+        cp.wait()
     row_ids = lax.broadcasted_iota(jnp.int32, (C, C), 0)
     clu_ids = lax.broadcasted_iota(jnp.int32, (C, T), 0)
 
@@ -118,71 +191,6 @@
     allowed = (qi <= kj) & (qi > kj - WINDOW_OF(T)) & (kj < (NS - s) * T)
     bias_t[...] = jnp.where(allowed, 0.0, -1e30)
 
-    pl.semaphore_wait(bar, (NX - 1) + 1 + (NY - 1) + (NZ - 1) + 4)
-
-    plan = ((k_in, kw, 2 * T), (v_in, vw, 2 * T), (q_in, qw, 0), (g_in, gw, 0))
-
-    def a2a_slices(i, ch, to):
-        src, dst, first = plan[i]
-        return (
-            src.at[:, pl.ds(pl.multiple_of(to * WD + ch * CW, CW), CW)],
-            dst.at[pl.ds(pl.multiple_of(first + x * RPD, RPD), RPD), pl.ds(ch * CW, CW)],
-        )
-
-    def a2a(i, ch, d):
-        to = lax.rem(x + d, NX)
-        return rc(*a2a_slices(i, ch, to), a2a_s.at[i, ch, d - 1], a2a_r.at[i, ch, d - 1], (s, to))
-
-    def own_copy(i, ch):
-        return pltpu.make_async_copy(*a2a_slices(i, ch, x), loc_sem.at[i, ch])
-
-    for ch in range(CH):
-        for i in range(4):
-            for d in range(1, NX):
-                a2a(i, ch, d).start()
-            own_copy(i, ch).start()
-
-    def a2a_wait(ch):
-        for i in range(4):
-            for d in range(1, NX):
-                a2a(i, ch, d).wait_recv()
-            own_copy(i, ch).wait()
-
-    def far(i, ch):
-        buf, first = plan[i][1], plan[i][2]
-        cols = pl.ds(ch * CW, CW)
-        return rc(
-            buf.at[pl.ds(first, T), cols], buf.at[pl.ds(2 * T - first, T), cols],
-            far_s.at[i, ch], far_r.at[i, ch], seq_off(2 if i < 2 else -2),
-        )
-
-    def near(i, ch):
-        buf = plan[i][1]
-        cols = pl.ds(ch * CW, CW)
-        first = 2 * T * (1 - c)
-        return rc(
-            buf.at[pl.ds(pl.multiple_of(first, T), T), cols], buf.at[pl.ds(T, T), cols],
-            near_s.at[i, ch], near_r.at[i, ch], at(z, y, 1 - c),
-        )
-
-    def send_near(ch, core, pair):
-        @pl.when(c == core)
-        def _():
-            for i in pair:
-                near(i, ch).start()
-
-    def halo_start(ch):
-        for i in range(4):
-            far(i, ch).start()
-        send_near(ch, 0, (0, 1))
-        send_near(ch, 1, (2, 3))
-
-    def halo_pass(ch):
-        for i in range(4):
-            far(i, ch).wait_recv()
-        send_near(ch, 1, (0, 1))
-        send_near(ch, 0, (2, 3))
-
     def c_copy(g, src, dst):
         return rc(src, dst, cl_s.at[g, 0], cl_r.at[g, 0], at(z, y, 1 - c))
 
@@ -196,6 +204,12 @@
 
     def z_loop(f):
         lax.fori_loop(1, NZ, lambda d, carry: (f(d), carry)[1], 0)
+
+    def q_copy(g, d, src, dst):
+        return rc(src, dst, co_s.at[g, d], co_r.at[g, d], at(z, y, 1 - c))
+
+    near_first = sorted(range(1, NY), key=lambda d: (min(d, NY - d), d))
+    far_first = near_first[::-1]
 
     cc0 = c_copy(0, cnt.at[0], cnt_c)
     cc0.start()
@@ -223,35 +237,41 @@
 
     for ch in range(CH):
         a2a_wait(ch)
-        halo_start(ch)
+        if ch < CH - 1:
+            halo_start(ch)
         lax.fori_loop(ch * HPC, (ch + 1) * HPC, add_sums, 0)
         if ch > 1:
             halo_pass(ch - 2)
     my_half = pl.ds(pl.multiple_of(c * HC, HC), HC)
     their_half = pl.ds(pl.multiple_of((1 - c) * HC, HC), HC)
-    cc1 = c_copy(1, sums.at[:, their_half, :], sums_c)
-    cc1.start()
-    cc1.wait_recv()
-
-    def add_half(p, carry):
-        v = sums[p, my_half, :] + sums_c[p]
-        half[p] = v
-        half_b[p] = v.astype(BF16)
-        return carry
-
-    lax.fori_loop(0, 2 * H, add_half, 0)
+    def half_rows(core, yy):
+        return pl.ds(pl.multiple_of(core * HC + yy * ZR, ZR), ZR)
 
     def y_rows(yy):
         return pl.ds(pl.multiple_of(yy * ZR, ZR), ZR)
 
+    def up(d):
+        return lax.rem(y + d, NY)
+
+    def down(d):
+        return lax.rem(y - d + NY, NY)
+
+    def c1(d):
+        return q_copy(0, d, sums.at[:, half_rows(1 - c, up(d)), :], sums_c.at[:, y_rows(up(d)), :])
+
     def y1(d):
-        return y_copy(1, d, half_b.at[:, y_rows(lax.rem(y + d, NY)), :], sums_y.at[d - 1])
-
-    for d in range(1, NY):
-        y1(d).start()
-
-    for ch in range(max(CH - 2, 0), CH):
-        halo_pass(ch)
+        return y_copy(1, d, half_b.at[:, y_rows(up(d)), :], sums_y.at[d - 1])
+
+    for d in far_first + [0]:
+        c1(d).start()
+    for d in far_first + [0]:
+        c1(d).wait_recv()
+        v = sums[:, half_rows(c, up(d)), :] + sums_c[:, y_rows(up(d)), :]
+        if d:
+            half_b[:, y_rows(up(d)), :] = v.astype(BF16)
+            y1(d).start()
+        else:
+            half[:, y_rows(y), :] = v
     for d in range(1, NY):
         y1(d).wait_recv()
     for p in range(2 * H):
@@ -267,6 +287,7 @@
 
     zb[...] = zs[...].astype(BF16)
     z_loop(lambda d: z1(d).start())
+    halo_start(CH - 1)
 
     own_keys = pl.ds(2 * T, T)
     lanes_t = lax.broadcasted_iota(jnp.int32, (T, HD), 1)
@@ -305,13 +326,13 @@
             st.at[:, pl.ds(0, T)], st.at[:, pl.ds(o * T, T)], st_s.at[o - 1], st_r.at[o - 1], seq_off(-o)
         )
 
-    for ch in range(CH):
+    for ch in range(CH - 2):
         for i in range(4):
             near(i, ch).wait_recv()
 
     sta[...] = jnp.zeros((T, HD), F32)
-    early = H * 5 // 8
-    lax.fori_loop(0, early, query_side, 0)
+    lax.fori_loop(0, (CH - 2) * HPC, query_side, 0)
+    halo_pass(CH - 2)
     z_loop(lambda d: z_copy(0, d, cnt.at[2], cnt_z.at[d - 1]).wait_recv())
     total = lax.fori_loop(0, NZ - 1, lambda d, t: t + cnt_z[d], cnt[2])
     count = pick(total, c * HC + y * ZR + z)
@@ -330,29 +351,42 @@
         return z_copy(2, d, agz.at[z], agz.at[z])
 
     z_loop(lambda d: z2(d).start())
-    lax.fori_loop(early, H, query_side, 0)
-    st[:, 0:T] = jnp.transpose(sta[...])[0 : 3 * H]
-    for o in (1, 2):
-        stat(o).start()
-
+    for i in range(4):
+        near(i, CH - 2).wait_recv()
+    lax.fori_loop((CH - 2) * HPC, (CH - 1) * HPC, query_side, 0)
+    halo_pass(CH - 1)
     z_loop(lambda d: z2(d).wait_recv())
     for i in range(NZ):
         tmp[i * 2 * H : (i + 1) * 2 * H, :] = agz[i].astype(F32)
     for p in range(2 * H):
         hy[p] = tmp[pl.ds(p, NZ, stride=2 * H), :].astype(BF16)
-    quarter = pl.ds(pl.multiple_of(c * HC + y * ZR, ZR), ZR)
-
-    def y2(d):
-        return y_copy(2, d, hy, cg.at[:, quarter, :])
-
-    for d in range(1, NY):
-        y2(d).start()
+    quarter = half_rows(c, y)
+    sides = (pl.ds(0, H), pl.ds(H, H))
+
+    def y2(side, d):
+        return y_copy(2 + 3 * side, d, hy.at[sides[side]], cg.at[sides[side], quarter, :])
+
+    def c2(side, d):
+        where = cg.at[sides[side], half_rows(c, down(d)), :]
+        return q_copy(1 + side, d, hy.at[sides[side]] if d == 0 else where, where)
+
+    for side in range(2):
+        for d in far_first:
+            y2(side, d).start()
+    c2(0, 0).start()
     cg[:, quarter, :] = hy[...]
-    for d in range(1, NY):
-        y2(d).wait_recv()
-    cc2 = c_copy(2, cg.at[:, my_half, :], cg.at[:, my_half, :])
-    cc2.start()
-    cc2.wait_recv()
+    for i in range(4):
+        near(i, CH - 1).wait_recv()
+    lax.fori_loop((CH - 1) * HPC, H, query_side, 0)
+    st[:, 0:T] = jnp.transpose(sta[...])[0 : 3 * H]
+    for o in (1, 2):
+        stat(o).start()
+
+    for d in near_first:
+        y2(0, d).wait_recv()
+        c2(0, d).start()
+    for d in range(NY):
+        c2(0, d).wait_recv()
 
     lanes_c = lax.broadcasted_iota(jnp.int32, (C, HD), 1)
     tops, masses = jnp.zeros((C, HD), F32), jnp.zeros((C, HD), F32)
@@ -366,29 +400,44 @@
         masses = jnp.where(lanes_c == h, jnp.sum(e, axis=1, keepdims=True), masses)
     pay[H] = tops
     pay[H + 1] = masses
-    cc3 = c_copy(3, pay.at[:, their_half, :], pay_c)
-    cc3.start()
-
-    cc3.wait_recv()
-    ma, mb = pay[H, my_half, :], pay_c[H]
-    mm_ = jnp.maximum(ma, mb)
-    fa, fb = jnp.exp(ma - mm_), jnp.exp(mb - mm_)
-    mass = pay[H + 1, my_half, :] * fa + pay_c[H + 1] * fb
-    pay_h[H] = mm_
-    pay_h[H + 1] = mass
-    for n, v in enumerate(split(mm_) + split(mass)):
-        pay_b[H + n] = v
-    for h in range(H):
-        v = pay[h, my_half, :] * fa[:, h : h + 1] + pay_c[h] * fb[:, h : h + 1]
-        pay_h[h] = v
-        pay_b[h] = v.astype(BF16)
+    def c3(d):
+        return q_copy(3, d, pay.at[:, half_rows(1 - c, up(d)), :], pay_c.at[:, y_rows(up(d)), :])
 
     def y3(d):
-        return y_copy(3, d, pay_b.at[:, y_rows(lax.rem(y + d, NY)), :], pay_y.at[d - 1])
-
-    for d in range(1, NY):
-        y3(d).start()
-
+        return y_copy(3, d, pay_b.at[:, y_rows(up(d)), :], pay_y.at[d - 1])
+
+    for d in far_first + [0]:
+        c3(d).start()
+    c2(1, 0).start()
+    for d in near_first:
+        y2(1, d).wait_recv()
+        c2(1, d).start()
+    for d in far_first + [0]:
+        c3(d).wait_recv()
+        mine_q, rows = half_rows(c, up(d)), y_rows(up(d))
+        ma, mb = pay[H, mine_q, :], pay_c[H, rows, :]
+        top = jnp.maximum(ma, mb)
+        fa, fb = jnp.exp(ma - top), jnp.exp(mb - top)
+        mass = pay[H + 1, mine_q, :] * fa + pay_c[H + 1, rows, :] * fb
+        if d:
+            for n, v in enumerate(split(top) + split(mass)):
+                pay_b[H + n, rows, :] = v
+        else:
+            pay_h[H, rows, :] = top
+            pay_h[H + 1, rows, :] = mass
+        for h in range(H):
+            v = pay[h, mine_q, :] * fa[:, h : h + 1] + pay_c[h, rows, :] * fb[:, h : h + 1]
+            if d:
+                pay_b[h, rows, :] = v.astype(BF16)
+            else:
+                pay_h[h, rows, :] = v
+        if d:
+            y3(d).start()
+
+    for o in (1, 2):
+        stat(o).wait_recv()
+    some = H * 3 // 8
+    lax.fori_loop(0, some, key_side, 0)
     for d in range(1, NY):
         y3(d).wait_recv()
     ms = [pay_h[H, y_rows(y), :]] + [join([pay_y[d, H + n] for n in range(3)]) for d in range(NY - 1)]
@@ -417,9 +466,7 @@
     z_loop(lambda d: z3(d).start())
     zr2[0:16, :] = zb2[pl.ds(pl.multiple_of(z * 16, 16), 16), :]
 
-    for o in (1, 2):
-        stat(o).wait_recv()
-    lax.fori_loop(0, H, key_side, 0)
+    lax.fori_loop(some, H, key_side, 0)
     z_loop(lambda d: z3(d).wait_recv())
     tmp[0 : NZ * 16, :] = zr2[...].astype(F32)
     mz = join([tmp[pl.ds(H + n, NZ, stride=16), :] for n in range(3)])
@@ -454,7 +501,30 @@
 
     z_loop(lambda d: z4(d).start())
     agz2[my_rows16, :] = blk[...]
-    z_loop(lambda d: z4(d).wait_recv())
+    for ch in range(CH):
+        for i in range(4):
+            for d in range(1, NX):
+                a2a(i, ch, d).wait_send()
+            far(i, ch).wait_send()
+            near(i, ch).wait_send()
+    for o in (1, 2):
+        stat(o).wait_send()
+    for d in range(1, NY):
+        y_copy(0, d, cnt.at[1], cnt_y.at[d - 1]).wait_send()
+        for cp in (y1(d), y2(0, d), y2(1, d), y3(d)):
+            cp.wait_send()
+    for d in range(NY):
+        for cp in (c1(d), c2(0, d), c2(1, d), c3(d)):
+            cp.wait_send()
+
+    def drain(d):
+        z_copy(0, d, cnt.at[2], cnt_z.at[d - 1]).wait_send()
+        z1(d).wait_send()
+        z2(d).wait_send()
+        z3(d).wait_send()
+
+    z_loop(drain)
+    z_loop(lambda d: z4(d).wait())
     tmp[0 : NZ * 16, :] = agz2[...].astype(F32)
     for p in range(H + 6):
         co[p, quarter, :] = tmp[pl.ds(p, NZ, stride=16), :].astype(BF16)
@@ -462,13 +532,20 @@
     def y4(d):
         return y_copy(4, d, co.at[:, quarter, :], co.at[:, quarter, :])
 
-    for d in range(1, NY):
+    def c4(d):
+        where = co.at[:, half_rows(c, down(d)), :]
+        return q_copy(4, d, where, where)
+
+    for d in far_first:
         y4(d).start()
-    for d in range(1, NY):
+    c4(0).start()
+    for d in near_first:
         y4(d).wait_recv()
-    cc4 = c_copy(4, co.at[:, my_half, :], co.at[:, my_half, :])
-    cc4.start()
-    cc4.wait_recv()
+        c4(d).start()
+    for d in range(NY):
+        c2(1, d).wait_recv()
+    for d in range(NY):
+        c4(d).wait_recv()
 
     lse = join([co[H + n] for n in range(3)])
     deltas = join([co[H + 3 + n] for n in range(3)])
@@ -481,31 +558,19 @@
         dk_out[:, cols] = (dkw[:, cols] + mm(dl, cg[h], TN)).astype(BF16)
         dv_out[:, cols] = (dvw[:, cols] + mm(w.astype(BF16), cg[H + h], TN)).astype(BF16)
 
-    for ch in range(CH):
-        for i in range(4):
-            for d in range(1, NX):
-                a2a(i, ch, d).wait_send()
-            far(i, ch).wait_send()
-            near(i, ch).wait_send()
-    for o in (1, 2):
-        stat(o).wait_send()
-    for cp in (cc1, cc2, cc3, cc4):
-        cp.wait_send()
     for d in range(1, NY):
-        y_copy(0, d, cnt.at[1], cnt_y.at[d - 1]).wait_send()
-        y1(d).wait_send()
-        y2(d).wait_send()
-        y3(d).wait_send()
         y4(d).wait_send()
-
-    def drain(d):
-        z_copy(0, d, cnt.at[2], cnt_z.at[d - 1]).wait_send()
-        z1(d).wait_send()
-        z2(d).wait_send()
-        z3(d).wait_send()
-        z4(d).wait_send()
-
-    z_loop(drain)
+    for d in range(NY):
+        c4(d).wait_send()
+
+
+def flush(*refs):
+    sem = refs[10]
+    copies = [pltpu.make_async_copy(refs[i], refs[5 + i], sem.at[i]) for i in range(5)]
+    for cp in copies:
+        cp.start()
+    for cp in copies:
+        cp.wait()
 
 
 def WINDOW_OF(tokens):
@@ -524,7 +589,7 @@
         HC, ZR = C // NC, NZ
         dims = (NX, NZ, NY, NC, H, T, HD, CH)
         V, D = pltpu.VMEM, pltpu.SemaphoreType.DMA
-        groups = 5
+        groups = 6
         scratch = [
             V((3 * T, WD), BF16), V((3 * T, WD), BF16), V((3 * T, WD), BF16), V((3 * T, WD), BF16),
             V((T, WD), F32), V((T, WD), F32), V((H, C, T), BF16),
@@ -540,22 +605,34 @@
             V((H + 2, HC, HD), F32), V((H + 6, HC, HD), BF16), V((NY - 1, H + 6, ZR, HD), BF16),
             V((NZ * 16, HD), F32), V((NZ * 16, HD), BF16), V((NZ * 16, HD), BF16),
             V((16, HD), BF16), V((NZ * 16, HD), BF16), V((H + 6, C, HD), BF16),
+            V((H, T), jnp.int32), V((H, C), jnp.int32),
             D((4, CH)), D((4, CH, NX - 1)), D((4, CH, NX - 1)), D((4, CH)), D((4, CH)),
             D((4, CH)), D((4, CH)), D((2,)), D((2,)), D((groups, NY + NZ - 1)), D((groups, NY + NZ - 1)),
+            D((5, NY)), D((5, NY)), D((2,)),
         ]
         wide = jax.ShapeDtypeStruct((T, WD), BF16)
-        hbm = pl.BlockSpec(memory_space=pl.ANY)
+        hbm = pl.BlockSpec(memory_space=pltpu.HBM)
         vmem = pl.BlockSpec(memory_space=pltpu.VMEM)
+        ins = (q, k, v, g, clusters, owner_slot)
         outs = pl.pallas_call(
             functools.partial(kernel, dims),
             out_shape=(wide, wide, wide, wide, jax.ShapeDtypeStruct((H, HD), BF16)),
-            in_specs=[hbm] * 4 + [vmem] * 2,
+            in_specs=[hbm] * 6,
             out_specs=(vmem,) * 5,
             scratch_shapes=scratch,
             compiler_params=pltpu.CompilerParams(
-                collective_id=0, has_side_effects=True, vmem_limit_bytes=60 * 1024 * 1024
+                collective_id=0, has_side_effects=True, vmem_limit_bytes=40 * 1024 * 1024
             ),
-        )(q, k, v, g, clusters, owner_slot)
+        )(*(pltpu.with_memory_space_constraint(a, pltpu.HBM) for a in ins))
+        small = jax.ShapeDtypeStruct((H, HD), BF16)
+        outs = pl.pallas_call(
+            flush,
+            out_shape=(wide, wide, wide, wide, small),
+            in_specs=[vmem] * 5,
+            out_specs=(hbm,) * 5,
+            scratch_shapes=[D((5,))],
+            compiler_params=pltpu.CompilerParams(vmem_limit_bytes=8 * 1024 * 1024),
+        )(*outs)
         return (*outs[:4], outs[4].reshape(H, 1, HD))
 
     rows = P(("seq", "head"), None)

time: 118 us -> 109 us (0.924)
  local copies, waits for them, and re-layouts: 5.76 us -> 0 us
  Pallas kernels: 112 us -> 108 us
    unnamed x13 -> x0, local copies, waits for them, and re-layouts: 5.76 us -> none
    pallas_call x1, Pallas kernels: 112 us -> 107 us  [body(): pl.pallas_call(functools.partial(kernel, dims), out_shape=(wide, wide, wi...]
    pallas_call x0 -> x1, Pallas kernels: none -> 1.36 us  [body(): pl.pallas_call(flush, out_shape=(wide, wide, wide, wide, small), in_specs...]
where the time goes in v3:
time: 109 us
  Pallas kernels  108 us (99%)
    pallas_call x1, Pallas kernels, body(): pl.pallas_call(functools.partial(kernel, dims), out_shape=(wide, wide, wi...  107 us

profile of v3, /device:TPU:1, one launch (start us, length us, event | category | flops | bytes accessed | tf_op | source)
XLA Modules:
  0.0 108.8 jit_solution(3986458243311384100)
XLA Ops:
  0.6 106.8 %shard_map.101 = (bf16[256,1024]{1,0:T(8,128)(2,1)S(1)}, bf16[256,1024]{1,0:T(8,128)(2,1)S(1)}, bf16[256,1024]{1,0:T(8,128)(2,1)S(1)}, bf16[256,1024]{1,0:T(8,128)(2,1)S(1)}, bf16[8,128]{1,0:T(8,128)(2,1)S(1)}) custom-call(bf16[64,4096]{1,0:T(8,128)(2,1)} %q_in.1, bf16[64,4096]{1,0:T(8,128)(2,1)} %k_in.1, bf16[64,4096]{1,0:T(8,128)(2,1)} %v_in.1, ...), custom_call_target="tpu_custom_call" | custom-call | tf_op jit(solution)/shard_map/pallas_call | solution.py:617
  107.4 1.4 %shard_map.102 = (bf16[256,1024]{1,0:T(8,128)(2,1)}, bf16[256,1024]{1,0:T(8,128)(2,1)}, bf16[256,1024]{1,0:T(8,128)(2,1)}, bf16[256,1024]{1,0:T(8,128)(2,1)}, bf16[8,128]{1,0:T(8,128)(2,1)}) custom-call(bf16[256,1024]{1,0:T(8,128)(2,1)S(1)} %get-tuple-element.15.refs_0_, bf16[256,1024]{1,0:T(8,128)(2,1)S(1)} %get-tuple-element.16.refs_1_, ...), custom_call_target="tpu_custom_call" | custom-call | tf_op jit(solution)/shard_map/pallas_call | solution.py:628

commit v4 on v3

--- a/solution.py
+++ b/solution.py
@@ -121,14 +121,16 @@
     def own_copy(i, ch):
         return pltpu.make_async_copy(*a2a_slices(i, ch, x), loc_sem.at[i, ch])
 
-    for ch in range(CH):
-        for i in range(4):
+    KV, QG = (0, 1), (2, 3)
+    order = [(KV, 0)] + [(QG, ch) for ch in range(CH)] + [(KV, ch) for ch in range(1, CH)]
+    for pair, ch in order:
+        for i in pair:
             for d in range(1, NX):
                 a2a(i, ch, d).start()
             own_copy(i, ch).start()
 
-    def a2a_wait(ch):
-        for i in range(4):
+    def a2a_wait(ch, pair):
+        for i in pair:
             for d in range(1, NX):
                 a2a(i, ch, d).wait_recv()
             own_copy(i, ch).wait()
@@ -236,12 +238,12 @@
         return carry
 
     for ch in range(CH):
-        a2a_wait(ch)
-        if ch < CH - 1:
-            halo_start(ch)
+        if ch == 0:
+            a2a_wait(0, KV)
+        a2a_wait(ch, QG)
+        if ch == 0:
+            halo_start(0)
         lax.fori_loop(ch * HPC, (ch + 1) * HPC, add_sums, 0)
-        if ch > 1:
-            halo_pass(ch - 2)
     my_half = pl.ds(pl.multiple_of(c * HC, HC), HC)
     their_half = pl.ds(pl.multiple_of((1 - c) * HC, HC), HC)
     def half_rows(core, yy):
@@ -287,7 +289,18 @@
 
     zb[...] = zs[...].astype(BF16)
     z_loop(lambda d: z1(d).start())
-    halo_start(CH - 1)
+    a2a_wait(1, KV)
+    halo_start(1)
+    halo_pass(0)
+
+    def near_wait(ch):
+        for i in range(4):
+            near(i, ch).wait_recv()
+
+    def queries(ch):
+        near_wait(ch)
+        lax.fori_loop(ch * HPC, (ch + 1) * HPC, query_side, 0)
+
 
     own_keys = pl.ds(2 * T, T)
     lanes_t = lax.broadcasted_iota(jnp.int32, (T, HD), 1)
@@ -310,29 +323,35 @@
         sta[...] = jnp.where(lanes_t == 2 * H + h, delta, old)
         return carry
 
-    def key_side(h, carry):
+    def key_side(n, h, carry):
         cols = head_cols(h)
         q, g = qw[:, cols], gw[:, cols]
         t = mm(kw[own_keys, cols], q, NT) * scale + bias_t[...]
-        p = jnp.exp(t - st[pl.ds(h, 1), :]) * st[pl.ds(H + h, 1), :]
+        p = jnp.exp(t - st[n, pl.ds(h, 1), :]) * st[n, pl.ds(H + h, 1), :]
         dp = mm(vw[own_keys, cols], g, NT)
-        ds = (p * (dp - st[pl.ds(2 * H + h, 1), :]) * scale).astype(BF16)
+        ds = (p * (dp - st[n, pl.ds(2 * H + h, 1), :]) * scale).astype(BF16)
         dkw[:, cols] = mm(ds, q, NN)
         dvw[:, cols] = mm(p.astype(BF16), g, NN)
         return carry
 
-    def stat(o):
+    def stat(n, o):
         return rc(
-            st.at[:, pl.ds(0, T)], st.at[:, pl.ds(o * T, T)], st_s.at[o - 1], st_r.at[o - 1], seq_off(-o)
+            st.at[n, :, pl.ds(0, T)], st.at[n, :, pl.ds(o * T, T)],
+            st_s.at[n, o - 1], st_r.at[n, o - 1], seq_off(-o),
         )
 
-    for ch in range(CH - 2):
-        for i in range(4):
-            near(i, ch).wait_recv()
+    def send_stats(n):
+        st[n, :, 0:T] = jnp.transpose(sta[...])[0 : 3 * H]
+        for o in (1, 2):
+            stat(n, o).start()
+
+    def keys(n, first, last):
+        for o in (1, 2):
+            stat(n, o).wait_recv()
+        lax.fori_loop(first * HPC, last * HPC, functools.partial(key_side, n), 0)
 
     sta[...] = jnp.zeros((T, HD), F32)
-    lax.fori_loop(0, (CH - 2) * HPC, query_side, 0)
-    halo_pass(CH - 2)
+    queries(0)
     z_loop(lambda d: z_copy(0, d, cnt.at[2], cnt_z.at[d - 1]).wait_recv())
     total = lax.fori_loop(0, NZ - 1, lambda d, t: t + cnt_z[d], cnt[2])
     count = pick(total, c * HC + y * ZR + z)
@@ -351,10 +370,11 @@
         return z_copy(2, d, agz.at[z], agz.at[z])
 
     z_loop(lambda d: z2(d).start())
-    for i in range(4):
-        near(i, CH - 2).wait_recv()
-    lax.fori_loop((CH - 2) * HPC, (CH - 1) * HPC, query_side, 0)
-    halo_pass(CH - 1)
+    for ch in range(2, CH):
+        a2a_wait(ch, KV)
+    halo_start(2)
+    halo_pass(1)
+    queries(1)
     z_loop(lambda d: z2(d).wait_recv())
     for i in range(NZ):
         tmp[i * 2 * H : (i + 1) * 2 * H, :] = agz[i].astype(F32)
@@ -375,13 +395,7 @@
             y2(side, d).start()
     c2(0, 0).start()
     cg[:, quarter, :] = hy[...]
-    for i in range(4):
-        near(i, CH - 1).wait_recv()
-    lax.fori_loop((CH - 1) * HPC, H, query_side, 0)
-    st[:, 0:T] = jnp.transpose(sta[...])[0 : 3 * H]
-    for o in (1, 2):
-        stat(o).start()
-
+    halo_pass(2)
     for d in near_first:
         y2(0, d).wait_recv()
         c2(0, d).start()
@@ -434,10 +448,8 @@
         if d:
             y3(d).start()
 
-    for o in (1, 2):
-        stat(o).wait_recv()
-    some = H * 3 // 8
-    lax.fori_loop(0, some, key_side, 0)
+    queries(2)
+    send_stats(0)
     for d in range(1, NY):
         y3(d).wait_recv()
     ms = [pay_h[H, y_rows(y), :]] + [join([pay_y[d, H + n] for n in range(3)]) for d in range(NY - 1)]
@@ -466,7 +478,8 @@
     z_loop(lambda d: z3(d).start())
     zr2[0:16, :] = zb2[pl.ds(pl.multiple_of(z * 16, 16), 16), :]
 
-    lax.fori_loop(some, H, key_side, 0)
+    halo_start(3)
+    keys(0, 0, 3)
     z_loop(lambda d: z3(d).wait_recv())
     tmp[0 : NZ * 16, :] = zr2[...].astype(F32)
     mz = join([tmp[pl.ds(H + n, NZ, stride=16), :] for n in range(3)])
@@ -501,14 +514,15 @@
 
     z_loop(lambda d: z4(d).start())
     agz2[my_rows16, :] = blk[...]
+    halo_pass(3)
+    queries(3)
+    send_stats(1)
     for ch in range(CH):
         for i in range(4):
             for d in range(1, NX):
                 a2a(i, ch, d).wait_send()
             far(i, ch).wait_send()
             near(i, ch).wait_send()
-    for o in (1, 2):
-        stat(o).wait_send()
     for d in range(1, NY):
         y_copy(0, d, cnt.at[1], cnt_y.at[d - 1]).wait_send()
         for cp in (y1(d), y2(0, d), y2(1, d), y3(d)):
@@ -539,6 +553,7 @@
     for d in far_first:
         y4(d).start()
     c4(0).start()
+    keys(1, 3, CH)
     for d in near_first:
         y4(d).wait_recv()
         c4(d).start()
@@ -562,6 +577,9 @@
         y4(d).wait_send()
     for d in range(NY):
         c4(d).wait_send()
+    for n in range(2):
+        for o in (1, 2):
+            stat(n, o).wait_send()
 
 
 def flush(*refs):
@@ -594,7 +612,7 @@
             V((3 * T, WD), BF16), V((3 * T, WD), BF16), V((3 * T, WD), BF16), V((3 * T, WD), BF16),
             V((T, WD), F32), V((T, WD), F32), V((H, C, T), BF16),
             V((T, WD), F32), V((T, 3 * T), F32), V((T, 3 * T), F32), V((T, HD), F32),
-            V((3 * H, 3 * T), F32),
+            V((2, 3 * H, 3 * T), F32),
             V((3, H, C), F32), V((H, C), F32), V((NY - 1, H, C), F32), V((NZ - 1, H, C), F32),
             V((2 * H, C, HD), F32), V((2 * H, HC, HD), F32), V((2 * H, HC, HD), F32),
             V((2 * H, HC, HD), BF16), V((NY - 1, 2 * H, ZR, HD), BF16), V((NZ * 2 * H, HD), F32),
@@ -607,7 +625,7 @@
             V((16, HD), BF16), V((NZ * 16, HD), BF16), V((H + 6, C, HD), BF16),
             V((H, T), jnp.int32), V((H, C), jnp.int32),
             D((4, CH)), D((4, CH, NX - 1)), D((4, CH, NX - 1)), D((4, CH)), D((4, CH)),
-            D((4, CH)), D((4, CH)), D((2,)), D((2,)), D((groups, NY + NZ - 1)), D((groups, NY + NZ - 1)),
+            D((4, CH)), D((4, CH)), D((2, 2)), D((2, 2)), D((groups, NY + NZ - 1)), D((groups, NY + NZ - 1)),
             D((5, NY)), D((5, NY)), D((2,)),
         ]
         wide = jax.ShapeDtypeStruct((T, WD), BF16)

time: 109 us -> 103 us (0.945)
  Pallas kernels: 108 us -> 102 us
    pallas_call x1, Pallas kernels: 107 us -> 100 us  [body(): pl.pallas_call(functools.partial(kernel, dims), out_shape=(wide, wide, wi...]
where the time goes in v4:
time: 103 us; the launch traced here: 102 us
  Pallas kernels  102 us (99%)
    pallas_call x1, Pallas kernels, body(): pl.pallas_call(functools.partial(kernel, dims), out_shape=(wide, wide, wi...  100 us

profile of v4, /device:TPU:1, one launch (start us, length us, event | category | flops | bytes accessed | tf_op | source)
XLA Modules:
  0.0 102.5 jit_solution(9859440803226777425)
XLA Ops:
  0.6 100.5 %shard_map.101 = (bf16[256,1024]{1,0:T(8,128)(2,1)S(1)}, bf16[256,1024]{1,0:T(8,128)(2,1)S(1)}, bf16[256,1024]{1,0:T(8,128)(2,1)S(1)}, bf16[256,1024]{1,0:T(8,128)(2,1)S(1)}, bf16[8,128]{1,0:T(8,128)(2,1)S(1)}) custom-call(bf16[64,4096]{1,0:T(8,128)(2,1)} %q_in.1, bf16[64,4096]{1,0:T(8,128)(2,1)} %k_in.1, bf16[64,4096]{1,0:T(8,128)(2,1)} %v_in.1, ...), custom_call_target="tpu_custom_call" | custom-call | tf_op jit(solution)/shard_map/pallas_call | solution.py:635
  101.1 1.4 %shard_map.102 = (bf16[256,1024]{1,0:T(8,128)(2,1)}, bf16[256,1024]{1,0:T(8,128)(2,1)}, bf16[256,1024]{1,0:T(8,128)(2,1)}, bf16[256,1024]{1,0:T(8,128)(2,1)}, bf16[8,128]{1,0:T(8,128)(2,1)}) custom-call(bf16[256,1024]{1,0:T(8,128)(2,1)S(1)} %get-tuple-element.15.refs_0_, bf16[256,1024]{1,0:T(8,128)(2,1)S(1)} %get-tuple-element.16.refs_1_, ...), custom_call_target="tpu_custom_call" | custom-call | tf_op jit(solution)/shard_map/pallas_call | solution.py:646

commit v5 on v4

--- a/solution.py
+++ b/solution.py
@@ -44,9 +44,9 @@
     dims, q_in, k_in, v_in, g_in, clus_in, slot_in, attn_out, dq_out, dk_out, dv_out, cent_out,
     qw, gw, kw, vw, dkw, dvw, mem, wout, bias, bias_t, sta, st,
     cnt, cnt_c, cnt_y, cnt_z,
-    sums, sums_c, half, half_b, sums_y, zs, zb, zr, own,
+    sums, sums_b, sums_c, half, half_b, sums_y, zs, zb, zr, own,
     agz, tmp, hy, cg,
-    lb, pay, pay_c, pay_h, pay_b, pay_y, zs2, zb2, zr2,
+    lb, dws, pay, pay_c, pay_h, pay_b, pay_y, zs2, zb2, zr2,
     blk, agz2, co, clus, slot,
     loc_sem, a2a_s, a2a_r, far_s, far_r, near_s, near_r, st_s, st_r, cl_s, cl_r, co_s, co_r, ids_sem,
 ):
@@ -233,8 +233,10 @@
 
     def add_sums(h, carry):
         m = mem[h]
-        sums[h] = mm(m, qw[own_rows, head_cols(h)], NN)
-        sums[H + h] = mm(m, gw[own_rows, head_cols(h)], NN)
+        for row, buf in ((h, qw), (H + h, gw)):
+            total = mm(m, buf[own_rows, head_cols(h)], NN)
+            sums[row] = total
+            sums_b[row] = total.astype(BF16)
         return carry
 
     for ch in range(CH):
@@ -259,7 +261,7 @@
         return lax.rem(y - d + NY, NY)
 
     def c1(d):
-        return q_copy(0, d, sums.at[:, half_rows(1 - c, up(d)), :], sums_c.at[:, y_rows(up(d)), :])
+        return q_copy(0, d, sums_b.at[:, half_rows(1 - c, up(d)), :], sums_c.at[:, y_rows(up(d)), :])
 
     def y1(d):
         return y_copy(1, d, half_b.at[:, y_rows(up(d)), :], sums_y.at[d - 1])
@@ -268,7 +270,7 @@
         c1(d).start()
     for d in far_first + [0]:
         c1(d).wait_recv()
-        v = sums[:, half_rows(c, up(d)), :] + sums_c[:, y_rows(up(d)), :]
+        v = sums[:, half_rows(c, up(d)), :] + sums_c[:, y_rows(up(d)), :].astype(F32)
         if d:
             half_b[:, y_rows(up(d)), :] = v.astype(BF16)
             y1(d).start()
@@ -395,7 +397,6 @@
             y2(side, d).start()
     c2(0, 0).start()
     cg[:, quarter, :] = hy[...]
-    halo_pass(2)
     for d in near_first:
         y2(0, d).wait_recv()
         c2(0, d).start()
@@ -426,6 +427,7 @@
     for d in near_first:
         y2(1, d).wait_recv()
         c2(1, d).start()
+    halo_pass(2)
     for d in far_first + [0]:
         c3(d).wait_recv()
         mine_q, rows = half_rows(c, up(d)), y_rows(up(d))
@@ -480,6 +482,10 @@
 
     halo_start(3)
     keys(0, 0, 3)
+    for d in range(NY):
+        c2(1, d).wait_recv()
+    for h in range(H):
+        dws[h] = mm(cg[H + h], vw[own_keys, head_cols(h)], NT)
     z_loop(lambda d: z3(d).wait_recv())
     tmp[0 : NZ * 16, :] = zr2[...].astype(F32)
     mz = join([tmp[pl.ds(H + n, NZ, stride=16), :] for n in range(3)])
@@ -558,8 +564,6 @@
         y4(d).wait_recv()
         c4(d).start()
     for d in range(NY):
-        c2(1, d).wait_recv()
-    for d in range(NY):
         c4(d).wait_recv()
 
     lse = join([co[H + n] for n in range(3)])
@@ -567,8 +571,7 @@
     for h in range(H):
         cols = head_cols(h)
         w = jnp.exp(lb[h] - pick(lse, h))
-        dw = mm(cg[H + h], vw[own_keys, cols], NT)
-        dl = (w * (dw - pick(deltas, h)) * scale).astype(BF16)
+        dl = (w * (dws[h] - pick(deltas, h)) * scale).astype(BF16)
         attn_out[:, cols] = (wout[:, cols] + mm(mem[h], co[h], TN)).astype(BF16)
         dk_out[:, cols] = (dkw[:, cols] + mm(dl, cg[h], TN)).astype(BF16)
         dv_out[:, cols] = (dvw[:, cols] + mm(w.astype(BF16), cg[H + h], TN)).astype(BF16)
@@ -614,12 +617,13 @@
             V((T, WD), F32), V((T, 3 * T), F32), V((T, 3 * T), F32), V((T, HD), F32),
             V((2, 3 * H, 3 * T), F32),
             V((3, H, C), F32), V((H, C), F32), V((NY - 1, H, C), F32), V((NZ - 1, H, C), F32),
-            V((2 * H, C, HD), F32), V((2 * H, HC, HD), F32), V((2 * H, HC, HD), F32),
+            V((2 * H, C, HD), F32), V((2 * H, C, HD), BF16), V((2 * H, HC, HD), BF16),
+            V((2 * H, HC, HD), F32),
             V((2 * H, HC, HD), BF16), V((NY - 1, 2 * H, ZR, HD), BF16), V((NZ * 2 * H, HD), F32),
             V((NZ * 2 * H, HD), BF16), V((NZ - 1, 2 * H, HD), BF16), V((2 * H, HD), F32),
             V((NZ, 2 * H, HD), BF16), V((NZ * 16, HD), F32), V((2 * H, NZ, HD), BF16),
             V((2 * H, C, HD), BF16),
-            V((H, C, T), F32), V((H + 2, C, HD), F32), V((H + 2, HC, HD), F32),
+            V((H, C, T), F32), V((H, C, T), F32), V((H + 2, C, HD), F32), V((H + 2, HC, HD), F32),
             V((H + 2, HC, HD), F32), V((H + 6, HC, HD), BF16), V((NY - 1, H + 6, ZR, HD), BF16),
             V((NZ * 16, HD), F32), V((NZ * 16, HD), BF16), V((NZ * 16, HD), BF16),
             V((16, HD), BF16), V((NZ * 16, HD), BF16), V((H + 6, C, HD), BF16),

time: 103 us -> 101 us (0.981)
    pallas_call x1, Pallas kernels: 100 us -> 99.3 us  [body(): pl.pallas_call(functools.partial(kernel, dims), out_shape=(wide, wide, wi...]
where the time goes in v5:
time: 101 us
  Pallas kernels  101 us (100%)
    pallas_call x1, Pallas kernels, body(): pl.pallas_call(functools.partial(kernel, dims), out_shape=(wide, wide, wi...  99.3 us

profile of v5, /device:TPU:1, one launch (start us, length us, event | category | flops | bytes accessed | tf_op | source)
XLA Modules:
  0.0 101.3 jit_solution(1094449146257007687)
XLA Ops:
  0.6 99.3 %shard_map.101 = (bf16[256,1024]{1,0:T(8,128)(2,1)S(1)}, bf16[256,1024]{1,0:T(8,128)(2,1)S(1)}, bf16[256,1024]{1,0:T(8,128)(2,1)S(1)}, bf16[256,1024]{1,0:T(8,128)(2,1)S(1)}, bf16[8,128]{1,0:T(8,128)(2,1)S(1)}) custom-call(bf16[64,4096]{1,0:T(8,128)(2,1)} %q_in.1, bf16[64,4096]{1,0:T(8,128)(2,1)} %k_in.1, bf16[64,4096]{1,0:T(8,128)(2,1)} %v_in.1, ...), custom_call_target="tpu_custom_call" | custom-call | tf_op jit(solution)/shard_map/pallas_call | solution.py:639
  99.9 1.4 %shard_map.102 = (bf16[256,1024]{1,0:T(8,128)(2,1)}, bf16[256,1024]{1,0:T(8,128)(2,1)}, bf16[256,1024]{1,0:T(8,128)(2,1)}, bf16[256,1024]{1,0:T(8,128)(2,1)}, bf16[8,128]{1,0:T(8,128)(2,1)}) custom-call(bf16[256,1024]{1,0:T(8,128)(2,1)S(1)} %get-tuple-element.15.refs_0_, bf16[256,1024]{1,0:T(8,128)(2,1)S(1)} %get-tuple-element.16.refs_1_, ...), custom_call_target="tpu_custom_call" | custom-call | tf_op jit(solution)/shard_map/pallas_call | solution.py:650
